TPU v7x, 32 devices: a whole 2x2x4 slice. The times are simulated.
32 devices in a mesh: groups: 2 (over y), resp: 4 (over z), section: 4 (over x, core).
Axes of the slice: x: 2, y: 2, z: 4, core: 2. Of those that a mesh axis runs over, the one named last changes fastest.
Arguments:
- completion_rows: bfloat16 [2, 8, 64, 4096], P(None, ('groups', 'resp')), parts along dimension 1, may hold values from -16 to 16
- prompt_pool: bfloat16 [4, 8, 64, 4096], P('section', ('groups', 'resp')), parts along dimension 1, may hold values from -16 to 16
- norm_gain: float32 [4, 4096], P('section'), may hold values from 0.5 to 1.5
- short_taps: float32 [4, 7, 4096], P('section'), may hold values from -2.4 to 2.4
- long_taps: float32 [4, 128, 256], P('section'), may hold values from -0.5 to 0.5
- score_head: float32 [4096], replicated, may hold values from -0.09375 to 0.09375
- live_lengths: int32 [2, 8], P(None, ('groups', 'resp')), parts along dimension 1, may hold values from 16 to 64, as said below
- prompt_owner: int32 [4], P('groups'), parts along dimension 0, may hold values from 0 to 3
- pair_index: int32 [2, 16, 2], P(None, 'groups'), parts along dimension 1, may hold values from 0 to 3
Outputs:
- scores: bfloat16 [2, 8], P(None, ('groups', 'resp')), parts along dimension 1
- gain_grad: float32 [4, 8192], P('section', 'groups'), parts along dimension 1
- short_grad: float32 [4, 14, 4096], P('section', 'groups'), parts along dimension 1
- long_grad: float32 [4, 256, 256], P('section', 'groups'), parts along dimension 1
There are 2 independent parts, one for each index of `groups`. A program takes and returns all parts, laid end to end along the dimension named above; an argument that names none is the same for every part. Nothing has to cross between parts.
Inputs may be any that keep to these rules, and one draw needn't show every extreme that they name: `live_lengths`: live rows of each completion, counted from its first row; in each microbatch one completion has all 64 rows live and another a quarter of 64. `pair_index`: the two members of a pair may coincide.
All inputs are finite; a program needn't handle non-finite values.
Results may differ from a plain program's by a relative error of at most 0.0097.
Values may be sent and summed in bfloat16 or wider, within the bound.
A program may use at most 256 MiB of HBM per device.

v0:
```python
import jax
import jax.numpy as jnp
from jax import lax
from jax.sharding import PartitionSpec as P


def spread(value, axis, root):
    mine = lax.axis_index(axis) == root
    return lax.psum(jnp.where(mine, value, jnp.zeros_like(value)), axis)


def from_behind(block, axis, distance):
    devices = range(lax.axis_size(axis))
    route = [(i - distance, i) for i in devices if i - distance in devices]
    return lax.ppermute(block, axis, route)


def lag_table(out_rows, all_rows, offset_rows, tap_total):
    lags = (
        offset_rows
        + jnp.arange(out_rows, dtype=jnp.int32)[:, None]
        - jnp.arange(all_rows, dtype=jnp.int32)[None, :]
    )
    return (lags[:, :, None] == jnp.arange(tap_total, dtype=jnp.int32)[None, None, :]).astype(
        jnp.float32
    )


def build_toeplitz(long_row, onehot):
    return jnp.einsum("tsj,jg->gts", onehot, long_row, precision=lax.Precision.HIGHEST)


def fold_toeplitz(toep_grad, onehot):
    return jnp.einsum("tsj,gts->jg", onehot, toep_grad, precision=lax.Precision.HIGHEST)


def filters_apply(joined, normed, short_row, toep, offset_rows):
    count_rows = joined.shape[0]
    channels = joined.shape[1]
    groups_here = toep.shape[0]
    tap_count = short_row.shape[0]
    padded = jnp.pad(normed, ((tap_count - 1, 0), (0, 0)))
    shorter = jnp.zeros_like(normed)
    for offset in range(tap_count):
        begin = tap_count - 1 - offset
        shorter = shorter + short_row[offset][None, :] * padded[begin : begin + count_rows]
    grouped = shorter.reshape(count_rows, groups_here, channels // groups_here)
    longer = jnp.einsum("gts,sgk->tgk", toep, grouped, precision=lax.Precision.HIGHEST)
    longer = longer.reshape(toep.shape[1], channels)
    return joined[offset_rows:] + normed[offset_rows:] * longer


def mixer(comp_rows, prompt_rows, gain_row, short_row, toep):
    joined = jnp.concatenate([prompt_rows, comp_rows], axis=0).astype(jnp.float32)
    factor = lax.rsqrt(jnp.mean(joined * joined, axis=1, keepdims=True) + 1e-06)
    normed = joined * factor * gain_row[None, :]
    return filters_apply(joined, normed, short_row, toep, prompt_rows.shape[0])


def pair_slopes(table, pair_index):
    labels = jnp.arange(table.shape[1], dtype=jnp.int32)
    winner = (pair_index[:, :, 0:1] == labels).astype(jnp.float32)
    loser = (pair_index[:, :, 1:2] == labels).astype(jnp.float32)
    margin = jnp.sum((winner - loser) * table[:, None, :], axis=2)
    weight = jax.nn.sigmoid(-margin)
    return jnp.sum((loser - winner) * weight[:, :, None], axis=1)


def cotangent_rows(slope_arg, head_arg, length_arg, count_rows):
    live = (jnp.arange(count_rows, dtype=jnp.int32) < length_arg).astype(jnp.float32)
    return slope_arg * live[:, None] * head_arg[None, :] / jnp.sqrt(length_arg.astype(jnp.float32))


def score_rows(section_out, head_arg, length_arg):
    per_row = jnp.dot(section_out.astype(jnp.float32), head_arg, precision=lax.Precision.HIGHEST)
    live = jnp.arange(section_out.shape[0], dtype=jnp.int32) < length_arg
    return jnp.sum(jnp.where(live, per_row, 0.0)) / jnp.sqrt(length_arg.astype(jnp.float32))


def put_slot(stored, fresh, chosen, active):
    former = lax.dynamic_index_in_dim(stored, chosen, 0, keepdims=False)
    return lax.dynamic_update_index_in_dim(stored, jnp.where(active, fresh, former), chosen, 0)


def sectioned_run(
    completion_rows,
    prompt_pool,
    norm_gain,
    short_taps,
    long_taps,
    score_head,
    live_lengths,
    prompt_owner,
    pair_index,
):
    sections = lax.axis_size("section")
    section_id = lax.axis_index("section")
    micro_count = completion_rows.shape[0]
    comp_len = completion_rows.shape[2]
    feat_width = completion_rows.shape[3]
    tick_count = sections + micro_count - 1
    gain_row = norm_gain[0]
    short_row = short_taps[0]
    long_row = long_taps[0]
    own_rows = completion_rows[:, 0]
    own_lengths = live_lengths[:, 0]
    local_prompt = prompt_pool[0, 0]
    prompt_len = local_prompt.shape[0]
    is_last = section_id == sections - 1
    is_first = section_id == 0
    batch_labels = jnp.arange(micro_count, dtype=jnp.int32)
    onehot = lag_table(comp_len, prompt_len + comp_len, prompt_len, long_row.shape[0])
    toep = build_toeplitz(long_row, onehot)
    prompt_store = jnp.zeros((micro_count,) + local_prompt.shape, local_prompt.dtype)
    saved_rows = jnp.zeros_like(own_rows)
    own_scores = jnp.zeros((micro_count,), jnp.float32)
    received = jnp.zeros((comp_len, feat_width), jnp.bfloat16)
    for moment in range(tick_count):
        slot_raw = moment - section_id
        active = (slot_raw >= 0) & (slot_raw < micro_count)
        chosen = jnp.clip(slot_raw, 0, micro_count - 1)
        fresh = lax.dynamic_index_in_dim(own_rows, chosen, 0, keepdims=False)
        current = jnp.where(is_first, fresh, received)
        saved_rows = put_slot(saved_rows, current, chosen, active)
        prompt_now = spread(local_prompt, "resp", prompt_owner[chosen])
        prompt_store = put_slot(prompt_store, prompt_now, chosen, active)

        def run_layer():
            return mixer(current, prompt_now, gain_row, short_row, toep).astype(jnp.bfloat16)

        def skip_layer():
            return jnp.zeros((comp_len, feat_width), jnp.bfloat16)

        output = lax.cond(active, run_layer, skip_layer)
        score_now = score_rows(output, score_head, own_lengths[chosen])
        own_scores = jnp.where(active & is_last & (batch_labels == chosen), score_now, own_scores)
        if moment + 1 < tick_count:
            received = from_behind(output, "section", 1)
    table = lax.all_gather(own_scores[:, None], "resp", axis=1, tiled=True)
    slopes = pair_slopes(table, pair_index)
    own_slope = lax.dynamic_slice_in_dim(slopes, lax.axis_index("resp"), 1, 1)[:, 0]
    rounded_scores = own_scores.astype(jnp.bfloat16)
    grad_gain = jnp.zeros_like(gain_row)
    grad_short = jnp.zeros_like(short_row)
    toep_acc = jnp.zeros_like(toep)
    received_grad = jnp.zeros((comp_len, feat_width), jnp.bfloat16)
    known = rounded_scores
    for moment in range(tick_count):
        slot_raw = moment - (sections - 1 - section_id)
        active = (slot_raw >= 0) & (slot_raw < micro_count)
        chosen = jnp.clip(slot_raw, 0, micro_count - 1)
        rows_now = lax.dynamic_index_in_dim(saved_rows, chosen, 0, keepdims=False)
        prompt_now = lax.dynamic_index_in_dim(prompt_store, chosen, 0, keepdims=False)
        head_grad = cotangent_rows(own_slope[chosen], score_head, own_lengths[chosen], comp_len)
        upstream = jnp.where(is_last, head_grad, received_grad.astype(jnp.float32))

        def pull_back():

            def local_layer(rows_var, gain_var, short_var, toep_var):
                return mixer(rows_var, prompt_now, gain_var, short_var, toep_var)

            primal, puller = jax.vjp(local_layer, rows_now, gain_row, short_row, toep)
            return puller(upstream)

        def nothing_back():
            return (
                jnp.zeros((comp_len, feat_width), jnp.bfloat16),
                jnp.zeros_like(gain_row),
                jnp.zeros_like(short_row),
                jnp.zeros_like(toep),
            )

        grad_rows, step_gain, step_short, step_toep = lax.cond(active, pull_back, nothing_back)
        toep_acc = toep_acc + step_toep
        grad_gain = grad_gain + step_gain
        grad_short = grad_short + step_short
        if moment + 1 < tick_count:
            received_grad, passed_scores = from_behind((grad_rows, known), "section", -1)
            known = jnp.where(is_last, rounded_scores, passed_scores)
    grad_long = fold_toeplitz(toep_acc, onehot)
    grad_gain, grad_short, grad_long = lax.psum((grad_gain, grad_short, grad_long), "resp")
    return (known[:, None], grad_gain[None], grad_short[None], grad_long[None])


def body(
    completion_rows,
    prompt_pool,
    norm_gain,
    short_taps,
    long_taps,
    score_head,
    live_lengths,
    prompt_owner,
    pair_index,
):
    results = sectioned_run(
        completion_rows,
        prompt_pool,
        norm_gain,
        short_taps,
        long_taps,
        score_head,
        live_lengths,
        prompt_owner,
        pair_index,
    )
    return results


def solution(mesh):
    placed = (
        P(None, ("groups", "resp"), None, None),
        P("section", ("groups", "resp"), None, None),
        P("section", None),
        P("section", None, None),
        P("section", None, None),
        P(),
        P(None, ("groups", "resp")),
        P("groups"),
        P(None, "groups", None),
    )
    return jax.shard_map(
        body,
        mesh=mesh,
        in_specs=placed,
        out_specs=(
            P(None, ("groups", "resp")),
            P("section", "groups"),
            P("section", "groups", None),
            P("section", "groups", None),
        ),
        check_vma=False,
    )
```

profile of v0, /device:TPU:0, one launch (start us, length us, event | category | flops | bytes accessed | tf_op | source)
XLA Modules:
  0.0 1085.8 jit_solution(16352563520942501082)
XLA Ops:
  29.0 94.0 %all-reduce.96.cloned.1.call-done = (bf16[64,4096]{1,0:T(8,128)(2,1)}, bf16[64,4096]{1,0:T(8,128)(2,1)}, bf16[64,4096]{1,0:T(8,128)(2,1)}, bf16[64,4096]{1,0:T(8,128)(2,1)}, bf16[64,4096]{1,0:T(8,128)(2,1)}) async-done(((bf16[64,4096]{1,0:T(8,128)(2,1)}, bf16[64,4096]{1,0:T(8,128)(2,1)}, bf16[64,4096]{1,0:T(8,128)(2,1)}, bf16[64,4096]{1,0:T(8,128)(2,1)}, bf16[64,4096]{1,0:T(8,128)(2,1)}), ...) | async-done | bytes 2621456 | tf_op jit(solution)/shard_map/psum | solution.py:9
  124.9 43.3 %conditional.10 = (bf16[64,4096]{0,1:T(8,128)(2,1)}) conditional(s32[]{:T(128)} %convert_element_type.230, () %tuple.107, (pred[]{:T(512)}, bf16[1,1,64,4096]{3,2,1,0:T(8,128)(2,1)S(1)}, bf16[64,4096]{1,0:T(8,128)(2,1)S(1)}, bf16[64,4096]{1,0:T(8,128)(2,1)}, f32[1,4096]{1,0:T(1,128)S(1)}, /*index=5*/f32[7,4096]{1,0:T(8,128)S(1)}, ...), branch_computations={%region_5.6_spmd, %region_6.8_spmd} | conditional | flops 418906240 | bytes 61179996 | solution.py:134
  141.5 8.7 copy.120
  150.2 15.8 %fusion.174 = f32[256,16,64]{2,1,0:T(8,128)S(1)} fusion(f32[128,256,16]{0,2,1:T(8,128)} %bitcast.617, f32[256,64,128]{2,1,0:T(8,128)} %copy.120), kind=kOutput, calls=%fused_computation.529 | convolution fusion | flops 402653184 | bytes 11534336 | tf_op jit(solution)/shard_map/cond/branch_1_fun/gts,sgk->tgk/dot_general | solution.py:48
  170.6 13.7 %collective-permute-start = (bf16[64,4096]{1,0:T(8,128)(2,1)}, bf16[64,4096]{1,0:T(8,128)(2,1)}, u32[]{:S(2)}, u32[]{:S(2)}) collective-permute-start(bf16[64,4096]{1,0:T(8,128)(2,1)} %copy.121), channel_id=1, source_target_pairs={{0,1},{1,2},{2,3},{4,5},{5,6},{6,7},{8,9},{9,10},{10,11},{12,13},{... | collective-permute-start | bytes 1572872 | tf_op jit(solution)/shard_map/ppermute | solution.py:15
  214.8 43.1 %conditional.11 = (bf16[64,4096]{0,1:T(8,128)(2,1)S(1)}) conditional(s32[]{:T(128)} %convert_element_type.229, () %tuple.106, (bf16[64,4096]{1,0:T(8,128)(2,1)}, bf16[64,4096]{1,0:T(8,128)(2,1)}, f32[1,4096]{1,0:T(1,128)S(1)}, f32[7,4096]{1,0:T(8,128)S(1)}, f32[256,64,128]{0,2,1:T(8,128)}) %tuple.377), branch_computations={%region_8.9_spmd, %region_9.11_spmd} | conditional | flops 418644096 | bytes 73238648 | solution.py:134
  232.1 8.7 copy.124
  240.9 15.8 %fusion.175 = f32[256,16,64]{2,1,0:T(8,128)S(1)} fusion(f32[128,256,16]{0,2,1:T(8,128)} %bitcast.618, f32[256,64,128]{2,1,0:T(8,128)} %copy.124), kind=kOutput, calls=%fused_computation.530 | convolution fusion | flops 402653184 | bytes 11534336 | tf_op jit(solution)/shard_map/cond/branch_1_fun/gts,sgk->tgk/dot_general | solution.py:48
  274.7 40.2 %collective-permute-start.2 = (bf16[64,4096]{1,0:T(8,128)(2,1)}, bf16[64,4096]{1,0:T(8,128)(2,1)}, u32[]{:S(2)}, u32[]{:S(2)}) collective-permute-start(bf16[64,4096]{1,0:T(8,128)(2,1)} %copy.129), channel_id=1, source_target_pairs={{0,1},{1,2},{2,3},{4,5},{5,6},{6,7},{8,9},{9,10},{10,11},{12,13},{... | collective-permute-start | bytes 1572872 | tf_op jit(solution)/shard_map/ppermute | solution.py:15
  360.8 15.7 %conditional.15 = (bf16[64,4096]{0,1:T(8,128)(2,1)}, f32[4096]{0:T(1024)S(1)}, f32[7,4096]{1,0:T(8,128)S(1)}, f32[256,64,128]{2,1,0:T(8,128)}) conditional(s32[]{:T(128)} %convert_element_type.237, () %tuple.113, (s32[]{:T(128)}, s32[2,1]{0,1:T(1,128)S(1)}, s32[64,1]{0,1:T(1,128)S(1)}, f32[2,4]{1,0:T(2,128)S(1)}, s32[]{:T(128)}, ...), branch_computations={%region_27.28_spmd, %region_28.39_spmd} | conditional | flops 1245062016 | bytes 171630560 | solution.py:173
  380.7 44.2 %collective-permute-done.8 = bf16[64,4096]{1,0:T(8,128)(2,1)} collective-permute-done((bf16[64,4096]{1,0:T(8,128)(2,1)S(1)}, bf16[64,4096]{1,0:T(8,128)(2,1)}, u32[]{:S(2)}, u32[]{:S(2)}) %collective-permute-start.8) | collective-permute-done | bytes 524320 | tf_op jit(solution)/shard_map/ppermute | solution.py:15
  427.0 15.6 %conditional.16 = (bf16[64,4096]{0,1:T(8,128)(2,1)}, f32[4096]{0:T(1024)S(1)}, f32[7,4096]{1,0:T(8,128)S(1)}, f32[256,64,128]{2,1,0:T(8,128)}) conditional(s32[]{:T(128)} %convert_element_type.240, () %tuple.115, (s32[]{:T(128)}, s32[2,1]{0,1:T(1,128)S(1)}, s32[64,1]{0,1:T(1,128)S(1)}, f32[2,4]{1,0:T(2,128)S(1)}, s32[]{:T(128)}, ...), branch_computations={%region_39.40_spmd, %region_40.51_spmd} | conditional | flops 1245062016 | bytes 174776288 | solution.py:173
  446.7 11.4 %collective-permute-done.9 = bf16[64,4096]{1,0:T(8,128)(2,1)} collective-permute-done((bf16[64,4096]{1,0:T(8,128)(2,1)S(1)}, bf16[64,4096]{1,0:T(8,128)(2,1)}, u32[]{:S(2)}, u32[]{:S(2)}) %collective-permute-start.9) | collective-permute-done | bytes 524320 | tf_op jit(solution)/shard_map/ppermute | solution.py:15
  460.2 15.6 %conditional.17 = (bf16[64,4096]{0,1:T(8,128)(2,1)}, f32[4096]{0:T(1024)S(1)}, f32[7,4096]{1,0:T(8,128)S(1)}, f32[256,64,128]{2,1,0:T(8,128)}) conditional(s32[]{:T(128)} %convert_element_type.242, () %tuple.117, (s32[]{:T(128)}, s32[2,1]{0,1:T(1,128)S(1)}, s32[64,1]{0,1:T(1,128)S(1)}, f32[2,4]{1,0:T(2,128)S(1)}, s32[]{:T(128)}, ...), branch_computations={%region_51.52_spmd, %region_52.0_spmd} | conditional | flops 1245062016 | bytes 174776288 | solution.py:173
  481.3 296.4 %collective-permute-done.10 = bf16[64,4096]{1,0:T(8,128)(2,1)} collective-permute-done((bf16[64,4096]{1,0:T(8,128)(2,1)S(1)}, bf16[64,4096]{1,0:T(8,128)(2,1)}, u32[]{:S(2)}, u32[]{:S(2)}) %collective-permute-start.10) | collective-permute-done | bytes 524320 | tf_op jit(solution)/shard_map/ppermute | solution.py:15
  779.7 101.2 %conditional.18 = (bf16[64,4096]{0,1:T(8,128)(2,1)}, f32[4096]{0:T(1024)S(1)}, f32[7,4096]{1,0:T(8,128)S(1)}, f32[256,64,128]{2,1,0:T(8,128)}) conditional(s32[]{:T(128)} %convert_element_type.244, () %tuple.119, (s32[]{:T(128)}, s32[2,1]{0,1:T(1,128)S(1)}, s32[64,1]{0,1:T(1,128)S(1)}, f32[2,4]{1,0:T(2,128)S(1)}, s32[]{:T(128)}, ...), branch_computations={%region_63.64_spmd, %region_64.0_spmd} | conditional | flops 1245062016 | bytes 174776288 | solution.py:173
  792.9 8.7 copy.165
  801.7 16.7 %fusion.187 = f32[256,16,64]{2,1,0:T(8,128)} fusion(f32[128,256,16]{0,2,1:T(8,128)} %bitcast.583, f32[256,64,128]{2,1,0:T(8,128)} %copy.165), kind=kOutput, calls=%fused_computation.542 | convolution fusion | flops 402653184 | bytes 11534336 | tf_op jit(solution)/shard_map/cond/branch_1_fun/jvp(gts,sgk->tgk)/dot_general | solution.py:48
  833.7 10.7 fusion.111
  844.4 11.8 %fusion.105 = (f32[4096]{0:T(1024)S(1)}, f32[4096]{0:T(1024)S(1)}, f32[4096]{0:T(1024)S(1)}, f32[4096]{0:T(1024)S(1)}, f32[4096]{0:T(1024)S(1)}, /*index=5*/f32[...) fusion(f32[256,16,128]{2,1,0:T(8,128)S(1)} %get-tuple-element.1, ...), kind=kLoop, calls=%fused_computation.333 | loop fusion | flops 9936896 | bytes 19087360 | tf_op jit(solution)/shard_map/cond/branch_1_fun/transpose(jvp())/reduce_sum | solution.py:46
  863.9 16.9 %fusion.188 = f32[256,64,128]{2,1,0:T(8,128)} fusion(f32[256,16,64]{2,1,0:T(8,128)} %bitcast.578, f32[128,256,16]{0,2,1:T(8,128)} %bitcast.584), kind=kOutput, calls=%fused_computation.543 | convolution fusion | flops 402653184 | bytes 11534336 | tf_op jit(solution)/shard_map/cond/branch_1_fun/transpose(jvp(gts,sgk->tgk))/dot_general | solution.py:48
  886.4 9.0 collective-permute-done.5
  907.4 99.8 %conditional.19 = (f32[4096]{0:T(1024)S(1)}, f32[7,4096]{1,0:T(8,128)S(1)}, f32[256,64,128]{2,1,0:T(8,128)}) conditional(s32[]{:T(128)} %convert_element_type.246, () %tuple.121, (s32[]{:T(128)}, bf16[2,64,4096]{1,2,0:T(8,128)(2,1)}, bf16[2,64,4096]{1,2,0:T(8,128)(2,1)}, s32[2,1]{0,1:T(1,128)}, s32[64,1]{0,1:T(1,128)}, ...), branch_computations={%region_75.76_spmd, %region_76.86_spmd} | conditional | flops 1244012800 | bytes 143633472 | solution.py:173
  925.1 8.8 copy.168
  933.9 16.7 %fusion.179 = f32[256,16,64]{2,1,0:T(8,128)} fusion(f32[128,256,16]{0,2,1:T(8,128)} %bitcast.587, f32[256,64,128]{2,1,0:T(8,128)} %copy.168), kind=kOutput, calls=%fused_computation.534 | convolution fusion | flops 402653184 | bytes 11534336 | tf_op jit(solution)/shard_map/cond/branch_1_fun/jvp(gts,sgk->tgk)/dot_general | solution.py:48
  960.9 10.6 fusion.125
  971.6 12.2 %fusion.119 = (f32[4096]{0:T(1024)}, f32[4096]{0:T(1024)}, f32[4096]{0:T(1024)}, f32[4096]{0:T(1024)}, f32[4096]{0:T(1024)}, /*index=5*/f32[4096]{0:T(1024)}, f3...) fusion(f32[256,16,128]{2,1,0:T(8,128)S(1)} %get-tuple-element.1, ...), kind=kLoop, calls=%fused_computation.392 | loop fusion | flops 9936896 | bytes 19087360 | tf_op jit(solution)/shard_map/cond/branch_1_fun/transpose(jvp())/reduce_sum | solution.py:46
  990.3 16.6 %fusion.180 = f32[256,64,128]{2,1,0:T(8,128)} fusion(f32[256,16,64]{2,1,0:T(8,128)} %bitcast.590, f32[128,256,16]{0,2,1:T(8,128)S(1)} %bitcast.588), kind=kOutput, calls=%fused_computation.535 | convolution fusion | flops 402653184 | bytes 11534336 | tf_op jit(solution)/shard_map/cond/branch_1_fun/transpose(jvp(gts,sgk->tgk))/dot_general | solution.py:48
  1009.1 19.7 %add_add_fusion.4 = f32[256,64,128]{2,1,0:T(8,128)} fusion(f32[256,64,128]{2,1,0:T(8,128)} %get-tuple-element.909, f32[256,64,128]{2,1,0:T(8,128)} %get-tuple-element.908, f32[256,64,128]{2,1,0:T(8,128)} %get-tuple-element.907, f32[256,64,128]{2,1,0:T(8,128)} %get-tuple-element.905, f32[256,64,128]{2,1,0:T(8,128)} %get-tuple-element.906), kind=kLoop, calls=%fused_computation.412 | loop fusion | flops 8388608 | bytes 50331648 | tf_op jit(solution)/shard_map/add | solution.py:174
  1028.9 13.8 %fusion.133 = f32[1,128,256]{2,1,0:T(8,128)} fusion(f32[256,64,128]{2,1,0:T(8,128)} %add_add_fusion.4, s32[64,128]{1,0:T(8,128)S(1)} %copy-done.89), kind=kOutput, calls=%fused_computation.418 | convolution fusion | flops 3222274048 | bytes 8552448 | tf_op jit(solution)/shard_map/tsj,gts->jg/dot_general | solution.py:34
  1044.0 17.1 %psum.61 = f32[1,4096]{1,0:T(1,128)} all-reduce(f32[1,4096]{1,0:T(1,128)S(1)} %bitcast.746), channel_id=1, replica_groups=mesh['groups'=2,'resp'=4,'section'=4] {'resp'}, use_global_device_ids=true, to_apply=%region_86.87 | all-reduce | flops 4096 | bytes 32768 | tf_op jit(solution)/shard_map/psum | solution.py:181
  1061.1 14.6 %all-reduce.94.cloned.1.call-done = (f32[1,7,4096]{2,0,1:T(1,128)}, f32[1,128,256]{2,1,0:T(8,128)}) async-done(((f32[1,7,4096]{2,0,1:T(1,128)}, f32[1,128,256]{2,1,0:T(8,128)}), (f32[1,7,4096]{2,0,1:T(1,128)}, f32[1,128,256]{2,1,0:T(8,128)})) %all-reduce.94.cloned.1.call-update) | async-done | bytes 245776 | tf_op jit(solution)/shard_map/psum | solution.py:181
  (350 shorter events, 275.7 us)
Async XLA Ops:
  7.2 16.1 %copy-start = (f32[1,128,256]{2,1,0:T(8,128)S(1)}, f32[1,128,256]{2,1,0:T(8,128)}, u32[]{:S(2)}) copy-start(f32[1,128,256]{2,1,0:T(8,128)} %param.33) | copy-start | bytes 393220
  7.2 115.8 %all-reduce.96.cloned.1.call-start = ((), (), s32[]{:S(2)}) async-start(), calls=%async_computation.1 | async-start | bytes 5242880 | tf_op jit(solution)/shard_map/psum | solution.py:9
  14.6 1061.1 %all-reduce.94.cloned.1.call-start = ((), (), s32[]{:S(2)}) async-start(), calls=%async_computation | async-start | bytes 491520 | tf_op jit(solution)/shard_map/psum | solution.py:181
  23.3 101.7 %copy-start.80 = (f32[1,4096]{1,0:T(1,128)S(1)}, f32[1,4096]{1,0:T(1,128)}, u32[]{:S(2)}) copy-start(f32[1,4096]{1,0:T(1,128)} %param.31) | copy-start | bytes 49156
  150.2 15.8 %copy-start.66 = (f32[128,4096]{0,1:T(8,128)S(1)}, f32[128,4096]{0,1:T(8,128)}, u32[]{:S(2)}) copy-start(f32[128,4096]{0,1:T(8,128)} %maximum_convert_fusion) | copy-start | bytes 6291460 | tf_op jit(solution)/shard_map/cond
  170.6 39.4 %collective-permute-start = (bf16[64,4096]{1,0:T(8,128)(2,1)}, bf16[64,4096]{1,0:T(8,128)(2,1)}, u32[]{:S(2)}, u32[]{:S(2)}) collective-permute-start(bf16[64,4096]{1,0:T(8,128)(2,1)} %copy.121), channel_id=1, source_target_pairs={{0,1},{1,2},{2,3},{4,5},{5,6},{6,7},{8,9},{9,10},{10,11},{12,13},{... | collective-permute-start | bytes 1572872 | tf_op jit(solution)/shard_map/ppermute | solution.py:15
  240.8 15.8 %copy-start.18 = (f32[128,4096]{0,1:T(8,128)S(1)}, f32[128,4096]{0,1:T(8,128)}, u32[]{:S(2)}) copy-start(f32[128,4096]{0,1:T(8,128)} %copy-done.17) | copy-start | bytes 6291460 | tf_op jit(solution)/shard_map/cond
  240.8 15.9 %copy-start.67 = (f32[128,4096]{0,1:T(8,128)S(1)}, f32[128,4096]{0,1:T(8,128)}, u32[]{:S(2)}) copy-start(f32[128,4096]{0,1:T(8,128)} %maximum_convert_fusion.1) | copy-start | bytes 6291460 | tf_op jit(solution)/shard_map/cond
  259.0 9.1 collective-permute-start.1
  274.7 47.3 %collective-permute-start.2 = (bf16[64,4096]{1,0:T(8,128)(2,1)}, bf16[64,4096]{1,0:T(8,128)(2,1)}, u32[]{:S(2)}, u32[]{:S(2)}) collective-permute-start(bf16[64,4096]{1,0:T(8,128)(2,1)} %copy.129), channel_id=1, source_target_pairs={{0,1},{1,2},{2,3},{4,5},{5,6},{6,7},{8,9},{9,10},{10,11},{12,13},{... | collective-permute-start | bytes 1572872 | tf_op jit(solution)/shard_map/ppermute | solution.py:15
  328.4 9.2 collective-permute-start.3
  341.3 15.0 %copy-start.81 = (bf16[1,64,4096]{1,2,0:T(8,128)(2,1)S(1)}, bf16[1,64,4096]{1,2,0:T(8,128)(2,1)}, u32[]{:S(2)}) copy-start(bf16[1,64,4096]{1,2,0:T(8,128)(2,1)} %copy.146) | copy-start | bytes 1572868
  356.3 423.4 %copy-start.118 = (f32[2,4]{1,0:T(2,128)}, f32[2,4]{1,0:T(2,128)S(1)}, u32[]{:S(2)}) copy-start(f32[2,4]{1,0:T(2,128)S(1)} %fusion.156) | copy-start | bytes 100
  360.8 418.9 %copy-start.114 = (f32[64,1]{0,1:T(1,128)}, f32[64,1]{0,1:T(1,128)S(1)}, u32[]{:S(2)}) copy-start(f32[64,1]{0,1:T(1,128)S(1)} %broadcast.837) | copy-start | bytes 772
  379.4 45.5 %collective-permute-start.8 = (bf16[64,4096]{1,0:T(8,128)(2,1)S(1)}, bf16[64,4096]{1,0:T(8,128)(2,1)}, u32[]{:S(2)}, u32[]{:S(2)}) collective-permute-start(bf16[64,4096]{1,0:T(8,128)(2,1)S(1)} %copy.157), channel_id=1, source_target_pairs={{1,0},{2,1},{3,2},{5,4},{6,5},{7,6},{9,8},{10,9},{11,10},{13,12},{... | collective-permute-start | bytes 1572872 | tf_op jit(solution)/shard_map/ppermute | solution.py:15
  445.4 12.7 %collective-permute-start.9 = (bf16[64,4096]{1,0:T(8,128)(2,1)S(1)}, bf16[64,4096]{1,0:T(8,128)(2,1)}, u32[]{:S(2)}, u32[]{:S(2)}) collective-permute-start(bf16[64,4096]{1,0:T(8,128)(2,1)S(1)} %copy.160), channel_id=1, source_target_pairs={{1,0},{2,1},{3,2},{5,4},{6,5},{7,6},{9,8},{10,9},{11,10},{13,12},{... | collective-permute-start | bytes 1572872 | tf_op jit(solution)/shard_map/ppermute | solution.py:15
  478.6 299.0 %collective-permute-start.10 = (bf16[64,4096]{1,0:T(8,128)(2,1)S(1)}, bf16[64,4096]{1,0:T(8,128)(2,1)}, u32[]{:S(2)}, u32[]{:S(2)}) collective-permute-start(bf16[64,4096]{1,0:T(8,128)(2,1)S(1)} %copy.163), channel_id=1, source_target_pairs={{1,0},{2,1},{3,2},{5,4},{6,5},{7,6},{9,8},{10,9},{11,10},{13,12},{... | collective-permute-start | bytes 1572872 | tf_op jit(solution)/shard_map/ppermute | solution.py:15
  480.0 405.1 %collective-permute-start.4 = (bf16[2]{0:T(256)(128)(2,1)S(1)}, bf16[2]{0:T(256)(128)(2,1)S(1)}, u32[]{:S(2)}, u32[]{:S(2)}) collective-permute-start(bf16[2]{0:T(256)(128)(2,1)S(1)} %fusion.160), channel_id=1, source_target_pairs={{1,0},{2,1},{3,2},{5,4},{6,5},{7,6},{9,8},{10,9},{11,10},{13,12},{... | collective-permute-start | bytes 20 | tf_op jit(solution)/shard_map/ppermute | solution.py:15
  844.4 11.8 %copy-start.40 = (bf16[128,4096]{0,1:T(8,128)(2,1)S(1)}, bf16[128,4096]{0,1:T(8,128)(2,1)}, u32[]{:S(2)}) copy-start(bf16[128,4096]{0,1:T(8,128)(2,1)} %copy-done.39) | copy-start | bytes 3145732 | tf_op jit(solution)/shard_map/cond
  883.8 22.1 %collective-permute-start.11 = (bf16[64,4096]{1,0:T(8,128)(2,1)S(1)}, bf16[64,4096]{1,0:T(8,128)(2,1)S(1)}, u32[]{:S(2)}, u32[]{:S(2)}) collective-permute-start(bf16[64,4096]{1,0:T(8,128)(2,1)S(1)} %copy.166), channel_id=1, source_target_pairs={{1,0},{2,1},{3,2},{5,4},{6,5},{7,6},{9,8},{10,9},{11,10},{13,12},{... | collective-permute-start | bytes 1572872 | tf_op jit(solution)/shard_map/ppermute | solution.py:15
  885.1 10.3 collective-permute-start.5
  895.4 8.6 collective-permute-start.6
  904.5 138.2 %collective-permute-start.7 = (bf16[2]{0:T(256)(128)(2,1)}, bf16[2]{0:T(256)(128)(2,1)}, u32[]{:S(2)}, u32[]{:S(2)}) collective-permute-start(bf16[2]{0:T(256)(128)(2,1)} %broadcast_select_fusion.1), channel_id=1, source_target_pairs={{1,0},{2,1},{3,2},{5,4},{6,5},{7,6},{9,8},{10,9},{11,10},{13,12},{... | collective-permute-start | bytes 20 | tf_op jit(solution)/shard_map/ppermute | solution.py:15
  907.4 99.8 %copy-start.84 = (f32[7,4096]{1,0:T(8,128)S(1)}, f32[7,4096]{1,0:T(8,128)}, u32[]{:S(2)}) copy-start(f32[7,4096]{1,0:T(8,128)} %copy-done.83) | copy-start | bytes 344068
  990.2 16.6 %copy-start.111 = (f32[4096]{0:T(1024)S(1)}, f32[4096]{0:T(1024)}, u32[]{:S(2)}) copy-start(f32[4096]{0:T(1024)} %fusion.116) | copy-start | bytes 49156 | tf_op jit(solution)/shard_map/cond
  1009.1 19.7 %copy-start.89 = (s32[64,128]{1,0:T(8,128)S(1)}, s32[64,128]{1,0:T(8,128)}, u32[]{:S(2)}) copy-start(s32[64,128]{1,0:T(8,128)} %copy-done.88) | copy-start | bytes 98308
  1028.8 15.1 %copy-start.104 = (f32[4096]{0:T(1024)S(1)}, f32[4096]{0:T(1024)}, u32[]{:S(2)}) copy-start(f32[4096]{0:T(1024)} %copy-done.103) | copy-start | bytes 49156
  1028.8 15.1 %copy-start.106 = (f32[4096]{0:T(1024)S(1)}, f32[4096]{0:T(1024)}, u32[]{:S(2)}) copy-start(f32[4096]{0:T(1024)} %copy-done.105) | copy-start | bytes 49156
  1028.8 15.1 %copy-start.108 = (f32[4096]{0:T(1024)S(1)}, f32[4096]{0:T(1024)}, u32[]{:S(2)}) copy-start(f32[4096]{0:T(1024)} %copy-done.107) | copy-start | bytes 49156
  1028.8 15.1 %copy-start.110 = (f32[4096]{0:T(1024)S(1)}, f32[4096]{0:T(1024)}, u32[]{:S(2)}) copy-start(f32[4096]{0:T(1024)} %copy-done.109) | copy-start | bytes 49156
  1028.9 15.1 %copy-start.113 = (f32[4096]{0:T(1024)S(1)}, f32[4096]{0:T(1024)}, u32[]{:S(2)}) copy-start(f32[4096]{0:T(1024)} %copy-done.112) | copy-start | bytes 49156
  1028.9 49.9 %copy-start.1 = (f32[1,128,256]{2,1,0:T(8,128)S(1)}, f32[1,128,256]{2,1,0:T(8,128)}, u32[]{:S(2)}) copy-start(f32[1,128,256]{2,1,0:T(8,128)} %param.33) | copy-start | bytes 393220
  (58 other events, 289.9 us)
Sparse Core Ops, SparseCore 0:
  14.7 108.2 all-reduce.95
  1042.8 32.8 all-reduce.93
where the time goes:
time: 1090 us
  waiting for transfers between devices  477 us (44%)
  other arithmetic  157 us (14%)
  matrix products  151 us (14%)
  local copies, waits for them, and re-layouts  148 us (14%)
  starting transfers between devices  68.4 us (6%)
  loops' own time  34.5 us (3%)
  blocking collectives  25.6 us (2%)
  between operations  24.9 us (2%)
    ppermute x12, waiting for transfers between devices, from_behind(): return lax.ppermute(block, axis, route)  368 us
    dot_general x8, matrix products, filters_apply(): jnp.einsum('gts,sgk->tgk', toep, grouped, precision=lax.Precision.HIGHEST)  120 us
    psum x1, waiting for transfers between devices, spread(): return lax.psum(jnp.where(mine, value, jnp.zeros_like(value)), axis)  94 us
    ppermute x12, starting transfers between devices, from_behind(): return lax.ppermute(block, axis, route)  68.4 us
    another operation x32, local copies, waits for them, and re-layouts  67.1 us
    add x4, other arithmetic, filters_apply(): shorter + short_row[offset][None, :] * padded[begin:begin + count_rows]  33.5 us
    another operation x5, loops' own time, sectioned_run(): lax.cond(active, pull_back, nothing_back)  33.2 us
    reduce_sum x2, other arithmetic, filters_apply(): short_row[offset][None, :] * padded[begin:begin + count_rows]  24 us
  transfers between devices with their start and end apart: 14, of which 7 were waited for; matrix products, arithmetic and copies ran while one was open for 27% of the time, Pallas kernels for 0%

commit v1 on v0

v1 whole, which is shorter than its diff:
```python
import functools

import jax
import jax.numpy as jnp
from jax import lax
from jax.experimental import pallas as pl
from jax.experimental.pallas import tpu as pltpu
from jax.sharding import PartitionSpec as P

LANES = 128
MESH = pl.DeviceIdType.MESH
F32 = jnp.float32
BF16 = jnp.bfloat16


def rows_to_line(block):
    line = jnp.sum(jnp.transpose(block), axis=0, keepdims=True)
    return jnp.broadcast_to(line, (8, LANES))


def line_to_rows(tile):
    return jnp.transpose(jnp.broadcast_to(tile[0:1], (LANES, LANES)))


def kernel(
    dims,
    direct,
    comp_ref,
    prompt_ref,
    gs_hbm,
    taps_hbm,
    chosen_ref,
    head_ref,
    pairs_ref,
    own_pairs_ref,
    live_ref,
    score_ref,
    tiles_ref,
    toep,
    toep_t,
    pool,
    chosen_rows,
    gs_ref,
    taps_ref,
    rows_in,
    short_out,
    long_out,
    fac_p,
    fac_c,
    upstream,
    partial,
    stat_acc,
    score_acc,
    prompt_acc,
    stat_out,
    stat_in,
    resp_out,
    resp_in,
    tiles_own,
    tiles_in,
    tiles_sum,
    local_sem,
    weight_sems,
    pool_send,
    pool_recv,
    stat_sems,
    resp_sems,
    part_sems,
    tile_send,
    tile_recv,
):
    sections, n_resp, micro, length, prompt_len, chans, per_group, width = dims
    groups = LANES // per_group
    blocks = chans // LANES
    group_rows = blocks * groups
    total = prompt_len + length
    me = lax.axis_index("section")
    me_resp = lax.axis_index("resp")
    own_lanes = pl.ds(pl.multiple_of(me * chans, chans), chans)

    def lane_slice(block):
        return pl.ds(pl.multiple_of(block * LANES, LANES), LANES)

    def head_slice(block):
        return pl.ds(pl.multiple_of(me * chans + block * LANES, LANES), LANES)

    def wide_slice(block):
        return pl.ds(pl.multiple_of(block * micro * LANES, LANES), micro * LANES)

    def loop(low, high, step_of):
        def run(index, carry):
            step_of(index)
            return carry

        lax.fori_loop(low, high, run, 0)

    def swap(axis, count, mine, out_ref, in_ref, sems):
        def copy(step):
            return pltpu.make_async_remote_copy(
                src_ref=out_ref,
                dst_ref=in_ref.at[mine],
                send_sem=sems.at[0, step],
                recv_sem=sems.at[1, step],
                device_id={axis: lax.rem(mine + step, count)},
                device_id_type=MESH,
            )

        loop(1, count, lambda step: copy(step).start())
        in_ref[mine] = out_ref[...]
        return lambda: loop(1, count, lambda step: copy(step).wait())

    def start_stats(slot, first, second):
        stat_out[slot, 0] = first
        stat_out[slot, 1] = second
        wait = swap(
            "section", sections, me, stat_out.at[slot], stat_in.at[slot], stat_sems.at[slot]
        )

        def finish():
            wait()
            return jnp.sum(stat_in[slot], axis=0)

        return finish

    def weight_copies(step):
        peer = lax.rem(me + step, sections)
        lanes = pl.ds(pl.multiple_of(peer * chans, chans), chans)
        rows = pl.ds(pl.multiple_of(peer * group_rows, group_rows), group_rows)
        return [
            pltpu.make_async_remote_copy(
                src_ref=source,
                dst_ref=target,
                send_sem=weight_sems.at[0, kind, step],
                recv_sem=weight_sems.at[1, kind, step],
                device_id={"section": peer},
                device_id_type=MESH,
            )
            for kind, source, target in (
                (0, gs_hbm.at[:, lanes], gs_ref.at[me]),
                (1, taps_hbm.at[rows, :], taps_ref.at[me]),
            )
        ]

    def start_weights(step):
        for copy in weight_copies(step):
            copy.start()

    def wait_weights(step):
        for copy in weight_copies(step):
            copy.wait()

    own_rows = pl.ds(pl.multiple_of(me * group_rows, group_rows), group_rows)
    local_copies = [
        pltpu.make_async_copy(comp_ref.at[:, own_lanes], rows_in.at[0], local_sem.at[0]),
        pltpu.make_async_copy(gs_hbm.at[:, own_lanes], gs_ref.at[me], local_sem.at[1]),
        pltpu.make_async_copy(taps_hbm.at[own_rows, :], taps_ref.at[me], local_sem.at[2]),
    ]

    def pool_copy(section_step, resp_step):
        peer = lax.rem(me + section_step, sections)
        lanes = pl.ds(pl.multiple_of(peer * chans, chans), chans)
        return pltpu.make_async_remote_copy(
            src_ref=prompt_ref.at[:, lanes],
            dst_ref=pool.at[me, me_resp],
            send_sem=pool_send.at[section_step, resp_step],
            recv_sem=pool_recv.at[me, me_resp],
            device_id={"section": peer, "resp": lax.rem(me_resp + resp_step, n_resp)},
            device_id_type=MESH,
        )

    def pool_arrival(s, r):
        return pltpu.make_async_remote_copy(
            src_ref=prompt_ref.at[:, own_lanes],
            dst_ref=pool.at[s, r],
            send_sem=pool_send.at[0, 0],
            recv_sem=pool_recv.at[s, r],
            device_id={"section": lax.rem(me + 1, sections)},
            device_id_type=MESH,
        )

    own_pool = (
        pltpu.make_async_copy(
            prompt_ref.at[:, own_lanes], pool.at[me, me_resp], pool_recv.at[me, me_resp]
        )
        if direct
        else None
    )

    def pool_steps(action):
        def each(step):
            @pl.when(step > 0)
            def _():
                action(pool_copy(step // n_resp, step % n_resp))

        loop(0, sections * n_resp, each)

    def start_pool(s):
        @pl.when(me == s)
        def _():
            own_pool.start()
            pool_steps(lambda copy: copy.start())

    def wait_pool(s):
        def each(r):
            mine = (s == me) & (r == me_resp)

            @pl.when(mine)
            def _():
                own_pool.wait()

            @pl.when(jnp.logical_not(mine))
            def _():
                pool_arrival(s, r).wait_recv()

        loop(0, n_resp, each)

    for copy in local_copies:
        copy.start()
    loop(1, sections, start_weights)
    if direct:
        start_pool(0)
    for copy in local_copies:
        copy.wait()

    def first_stats(block):
        wide = rows_in[0, :, lane_slice(block)].astype(F32)
        stat_acc[...] += wide * wide

    stat_acc[...] = jnp.zeros_like(stat_acc)
    loop(0, blocks, first_stats)
    loop(1, sections, wait_weights)

    t_row = lax.broadcasted_iota(jnp.int32, (length, LANES), 0)
    s_lane = lax.broadcasted_iota(jnp.int32, (length, LANES), 1)
    keep = s_lane <= prompt_len + t_row
    s_row = lax.broadcasted_iota(jnp.int32, (total, LANES), 0)
    t_lane = lax.broadcasted_iota(jnp.int32, (total, LANES), 1)
    keep_t = s_row <= prompt_len + t_lane

    def build(s, block):
        rows = pl.ds(pl.multiple_of(block * groups, groups), groups)
        both = taps_ref[s, rows, :]
        flipped, plain = both[:, :LANES], both[:, LANES:]
        for g in range(groups):
            base = pl.multiple_of((block * groups + g) * length, length)
            wide = jnp.broadcast_to(flipped[g : g + 1], (length, LANES))
            wide = pltpu.roll(wide, prompt_len, 1, stride=1, stride_axis=0)
            wide = jnp.where(keep, wide, 0.0)
            high = wide.astype(BF16)
            low = (wide - high.astype(F32)).astype(BF16)
            toep[s, pl.ds(base, length), :] = jnp.concatenate([high, high, low], axis=1)
            base = pl.multiple_of((block * groups + g) * total, total)
            wide = jnp.broadcast_to(plain[g : g + 1], (total, LANES))
            wide = pltpu.roll(wide, prompt_len, 1, stride=1, stride_axis=0)
            toep_t[s, pl.ds(base, total), :] = jnp.where(keep_t, wide, 0.0).astype(BF16)

    def choose(s, block):
        lanes = lane_slice(block)
        for m in range(micro):
            rows = slice(m * prompt_len, (m + 1) * prompt_len)
            if direct:
                picked = jnp.zeros((prompt_len, LANES), F32)
                for r in range(n_resp):
                    flag = chosen_ref[m * n_resp + r : m * n_resp + r + 1, :] > 0.5
                    picked = jnp.where(flag, pool[s, r, :, lanes].astype(F32), picked)
                chosen_rows[s, rows, lanes] = picked.astype(BF16)
            else:
                picked = prompt_ref[s, rows, lanes].astype(F32)
                chosen_rows[s, rows, lanes] = prompt_ref[s, rows, lanes]
            prompt_acc[rows, :] += picked * picked

    row_id = lax.broadcasted_iota(jnp.int32, (total, LANES), 0)
    wide_group = (
        lax.broadcasted_iota(jnp.int32, (1, micro * LANES), 1) % LANES
    ) // per_group
    tap_count = gs_ref.shape[1] - 1

    def pick(stacked, rows):
        out = stacked[0:rows]
        for g in range(1, groups):
            out = jnp.where(wide_group == g, stacked[g * rows : (g + 1) * rows], out)
        return out

    def joined_rows(s, m, lanes):
        rows_p = slice(m * prompt_len, (m + 1) * prompt_len)
        rows_c = slice(m * length, (m + 1) * length)
        joined = jnp.concatenate(
            [chosen_rows[s, rows_p, lanes].astype(F32), rows_in[s, rows_c, lanes].astype(F32)],
            axis=0,
        )
        factor = jnp.concatenate([fac_p[s, rows_p, :], fac_c[s, rows_c, :]], axis=0)
        return joined, factor

    def forward(s, carry):
        if direct:
            wait_pool(s)
            start_pool(s + 1)
        prompt_acc[...] = jnp.zeros_like(prompt_acc)
        loop(0, blocks, lambda block: choose(s, block))
        finish = start_stats(s, rows_to_line(stat_acc[...]), rows_to_line(prompt_acc[...]))
        loop(0, blocks, lambda block: build(s, block))
        sums = finish()
        fac_c[s] = lax.rsqrt(line_to_rows(sums[0]) * (1.0 / width) + 1e-06)
        fac_p[s] = lax.rsqrt(line_to_rows(sums[1]) * (1.0 / width) + 1e-06)
        stat_acc[...] = jnp.zeros_like(stat_acc)
        score_acc[...] = jnp.zeros_like(score_acc)

        def run(block, carry):
            lanes = lane_slice(block)
            wide = wide_slice(block)
            gs = gs_ref[s, :, lanes]
            parts, lows, saved = [], [], []
            for m in range(micro):
                joined, factor = joined_rows(s, m, lanes)
                normed = joined * factor * gs[0:1]
                shorter = normed * gs[1:2]
                for j in range(1, tap_count):
                    moved = jnp.where(row_id >= j, pltpu.roll(normed, j, 0), 0.0)
                    shorter = shorter + moved * gs[1 + j : 2 + j]
                high = shorter.astype(BF16)
                parts.append(high)
                lows.append((shorter - high.astype(F32)).astype(BF16))
                saved.append((joined[prompt_len:], normed[prompt_len:]))
            high = jnp.concatenate(parts, axis=1)
            short_out[s, :, wide] = high
            rhs = jnp.concatenate([high, jnp.concatenate(lows, axis=1), high], axis=0)
            base = pl.multiple_of(block * groups * length, groups * length)
            stacked = jnp.dot(
                toep[s, pl.ds(base, groups * length), :], rhs, preferred_element_type=F32
            )
            longer_all = pick(stacked, length)
            for m in range(micro):
                rows = slice(m * length, (m + 1) * length)
                longer = longer_all[:, m * LANES : (m + 1) * LANES]
                long_out[s, rows, lanes] = longer
                mixed = (saved[m][0] + saved[m][1] * longer).astype(BF16)
                rows_in[s + 1, rows, lanes] = mixed
                mixed = mixed.astype(F32)
                stat_acc[rows, :] += mixed * mixed
                score_acc[rows, :] += mixed * head_ref[0:1, head_slice(block)]
            return carry

        lax.fori_loop(0, blocks, run, 0)

        return carry

    lax.fori_loop(0, sections, forward, 0)

    tile_rows = []
    for m in range(micro):
        rows = slice(m * length, (m + 1) * length)
        line = jnp.sum(score_acc[rows, :] * live_ref[rows, :], axis=0, keepdims=True)
        tile_rows.append(jnp.broadcast_to(jnp.sum(line, axis=1, keepdims=True), (1, LANES)))
    tile_rows.append(jnp.zeros((8 - micro, LANES), F32))
    score_tile = jnp.concatenate(tile_rows, axis=0)
    own_score = start_stats(sections, score_tile, score_tile)()[0]
    score_ref[...] = own_score
    resp_out[...] = own_score
    swap("resp", n_resp, me_resp, resp_out, resp_in, resp_sems)()
    margin = jnp.sum(resp_in[...] * pairs_ref[...], axis=0)
    weight = 1.0 / (1.0 + jnp.exp(margin))
    slopes = -jnp.sum(own_pairs_ref[...] * weight, axis=1, keepdims=True)

    def seed(block, carry):
        lanes = lane_slice(block)
        for m in range(micro):
            rows = slice(m * length, (m + 1) * length)
            upstream[rows, lanes] = live_ref[rows, :] * slopes[m : m + 1] * head_ref[0:1, head_slice(block)]
        return carry

    lax.fori_loop(0, blocks, seed, 0)

    keep_pair = total - 1 - s_lane <= prompt_len + t_row
    reverse = (
        lax.broadcasted_iota(jnp.int32, (total, total), 0)
        + lax.broadcasted_iota(jnp.int32, (total, total), 1)
        == total - 1
    )
    reverse = jnp.where(reverse, 1.0, 0.0).astype(BF16)

    share = 2 * blocks // n_resp

    def part_slice(r):
        return pl.ds(r * share, share)

    def part_steps(s, action):
        def each(step):
            peer = lax.rem(me_resp + step, n_resp)
            action(
                pltpu.make_async_remote_copy(
                    src_ref=tiles_own.at[s, part_slice(peer)],
                    dst_ref=tiles_in.at[s, me_resp],
                    send_sem=part_sems.at[0, s, step],
                    recv_sem=part_sems.at[1, s, step],
                    device_id={"resp": peer},
                    device_id_type=MESH,
                )
            )

        loop(1, n_resp, each)

    def tile_copy(s, step, k, r):
        return pltpu.make_async_remote_copy(
            src_ref=tiles_sum.at[s],
            dst_ref=tiles_ref.at[k, r],
            send_sem=tile_send.at[s, step],
            recv_sem=tile_recv.at[k, r],
            device_id={"section": s, "resp": lax.rem(me_resp + step, n_resp)},
            device_id_type=MESH,
        )

    def tile_steps(s, action):
        def each(step):
            @pl.when(jnp.logical_not((s == me) & (step == 0)))
            def _():
                action(tile_copy(s, step, me, me_resp))

        loop(0, n_resp, each)

    def backward(step, carry):
        s = sections - 1 - step
        stat_acc[...] = jnp.zeros_like(stat_acc)

        def run(block, carry):
            lanes = lane_slice(block)
            wide = wide_slice(block)
            gs = gs_ref[s, :, lanes]
            parts, saved = [], []
            for m in range(micro):
                rows = slice(m * length, (m + 1) * length)
                joined, factor = joined_rows(s, m, lanes)
                scaled = joined * factor
                normed = scaled * gs[0:1]
                above = upstream[rows, lanes]
                parts.append((above * normed[prompt_len:]).astype(BF16))
                saved.append((joined[prompt_len:], scaled, normed, above))
            d_long = jnp.concatenate(parts, axis=1)
            base = pl.multiple_of(block * groups * total, groups * total)
            stacked = jnp.dot(
                toep_t[s, pl.ds(base, groups * total), :][:, :length],
                d_long,
                preferred_element_type=F32,
            )
            d_short_all = pick(stacked, total)
            turned = jnp.dot(reverse, short_out[s, :, wide], preferred_element_type=F32)
            d_wide = d_long.astype(F32)
            masked = jnp.concatenate(
                [
                    jnp.where(wide_group == g, d_wide, 0.0).astype(BF16)
                    for g in range(groups)
                ],
                axis=0,
            )
            pairs = lax.dot_general(
                masked,
                turned.astype(BF16),
                (((1,), (1,)), ((), ())),
                preferred_element_type=F32,
            )
            lines = []
            for g in range(groups):
                one = jnp.where(keep_pair, pairs[g * length : (g + 1) * length], 0.0)
                one = pltpu.roll(one, LANES + 1 - length, 1, stride=1, stride_axis=0)
                lines.append(jnp.sum(one, axis=0, keepdims=True))
            tiles_own[s, 2 * block + 1] = jnp.concatenate(lines, axis=0)
            grads = [jnp.zeros((1, LANES), F32)] * (tap_count + 1)
            for m in range(micro):
                rows = slice(m * length, (m + 1) * length)
                joined_c, scaled, normed, above = saved[m]
                d_short = d_short_all[:, m * LANES : (m + 1) * LANES]
                d_normed = d_short * gs[1:2]
                grads[1] = grads[1] + jnp.sum(d_short * normed, axis=0, keepdims=True)
                for j in range(1, tap_count):
                    moved = jnp.where(
                        row_id < total - j, pltpu.roll(d_short, total - j, 0), 0.0
                    )
                    d_normed = d_normed + moved * gs[1 + j : 2 + j]
                    grads[1 + j] = grads[1 + j] + jnp.sum(
                        moved * normed, axis=0, keepdims=True
                    )
                direct = above * long_out[s, rows, lanes]
                d_normed = jnp.concatenate(
                    [d_normed[:prompt_len], d_normed[prompt_len:] + direct], axis=0
                )
                grads[0] = grads[0] + jnp.sum(d_normed * scaled, axis=0, keepdims=True)
                inner = d_normed[prompt_len:] * gs[0:1]
                partial[rows, lanes] = inner
                stat_acc[rows, :] += inner * joined_c
            tiles_own[s, 2 * block] = jnp.concatenate(grads, axis=0)
            return carry

        lax.fori_loop(0, blocks, run, 0)

        if direct:
            part_steps(s, lambda copy: copy.start())
            parts_in = tiles_in.at[s]
            parts_in[me_resp] = tiles_own[s, part_slice(me_resp)]

        @pl.when(s > 0)
        def _():
            line = rows_to_line(stat_acc[...])
            all_sums = start_stats(sections + 1 + step, line, line)()[0]
            factor = fac_c[s]
            pull = line_to_rows(all_sums) * (1.0 / width) * factor * factor * factor

            def finish(block, carry):
                lanes = lane_slice(block)
                grad = (
                    upstream[:, lanes]
                    + factor * partial[:, lanes]
                    - rows_in[s, :, lanes].astype(F32) * pull
                )
                upstream[:, lanes] = grad.astype(BF16).astype(F32)
                return carry

            lax.fori_loop(0, blocks, finish, 0)

        if direct:
            part_steps(s, lambda copy: copy.wait())
            tiles_sum[s] = jnp.sum(tiles_in[s], axis=0)

            @pl.when(s == me)
            def _():
                tiles_ref[me, me_resp] = tiles_sum[s]

            tile_steps(s, lambda copy: copy.start())

        return carry

    lax.fori_loop(0, sections, backward, 0)

    if direct:
        pool_steps(lambda copy: copy.wait_send())
        loop(0, sections, lambda s: tile_steps(s, lambda copy: copy.wait_send()))

        def arrive(step):
            k, r = step // n_resp, step % n_resp

            @pl.when(jnp.logical_not((k == me) & (r == me_resp)))
            def _():
                tile_copy(0, 0, k, r).wait_recv()

        loop(0, sections * n_resp, arrive)
    else:
        tiles_ref[...] = tiles_own[...]


def run_kernel(dims, direct, *arrays):
    sections, n_resp, micro, length, prompt_len, chans, per_group, width = dims
    rows = micro * length
    total = prompt_len + length
    group_total = chans // per_group
    tile = (8, LANES)
    tiles = 2 * chans // LANES
    share = tiles // n_resp if direct else 1
    ranks = n_resp if direct else 1
    vmem = pl.BlockSpec(memory_space=pltpu.VMEM)
    hbm = pl.BlockSpec(memory_space=pl.ANY)
    tiles_shape = (sections, n_resp, share) if direct else (sections, tiles)
    return pl.pallas_call(
        functools.partial(kernel, dims, direct),
        out_shape=(
            jax.ShapeDtypeStruct(tile, F32),
            jax.ShapeDtypeStruct(tiles_shape + tile, F32),
        ),
        in_specs=[hbm, hbm if direct else vmem, hbm, hbm] + [vmem] * (len(arrays) - 4),
        out_specs=(vmem,) * 2,
        scratch_shapes=[
            pltpu.VMEM((sections, group_total * length, 3 * LANES), BF16),
            pltpu.VMEM((sections, group_total * total, LANES), BF16),
            pltpu.VMEM((sections, ranks, prompt_len, chans), BF16),
            pltpu.VMEM((sections, micro * prompt_len, chans), BF16),
            pltpu.VMEM((sections, 8, chans), F32),
            pltpu.VMEM((sections, group_total, 2 * LANES), F32),
            pltpu.VMEM((sections + 1, rows, chans), BF16),
            pltpu.VMEM((sections, total, micro * chans), BF16),
            pltpu.VMEM((sections, rows, chans), F32),
            pltpu.VMEM((sections, micro * prompt_len, LANES), F32),
            pltpu.VMEM((sections, rows, LANES), F32),
            pltpu.VMEM((rows, chans), F32),
            pltpu.VMEM((rows, chans), F32),
            pltpu.VMEM((rows, LANES), F32),
            pltpu.VMEM((rows, LANES), F32),
            pltpu.VMEM((micro * prompt_len, LANES), F32),
            pltpu.VMEM((2 * sections, 2) + tile, F32),
            pltpu.VMEM((2 * sections, sections, 2) + tile, F32),
            pltpu.VMEM(tile, F32),
            pltpu.VMEM((n_resp,) + tile, F32),
            pltpu.VMEM((sections, tiles) + tile, F32),
            pltpu.VMEM((sections, ranks, share) + tile, F32),
            pltpu.VMEM((sections, share) + tile, F32),
            pltpu.SemaphoreType.DMA((3,)),
            pltpu.SemaphoreType.DMA((2, 2, sections)),
            pltpu.SemaphoreType.DMA((sections, ranks)),
            pltpu.SemaphoreType.DMA((sections, ranks)),
            pltpu.SemaphoreType.DMA((2 * sections, 2, sections)),
            pltpu.SemaphoreType.DMA((2, n_resp)),
            pltpu.SemaphoreType.DMA((2, sections, ranks)),
            pltpu.SemaphoreType.DMA((sections, ranks)),
            pltpu.SemaphoreType.DMA((sections, ranks)),
        ],
        compiler_params=pltpu.CompilerParams(
            has_side_effects=True, vmem_limit_bytes=56 * 1024 * 1024
        ),
    )(*arrays)


def body(
    completion_rows,
    prompt_pool,
    norm_gain,
    short_taps,
    long_taps,
    score_head,
    live_lengths,
    prompt_owner,
    pair_index,
):
    sections = lax.axis_size("section")
    n_resp = lax.axis_size("resp")
    me_resp = lax.axis_index("resp")
    micro, _, length, width = completion_rows.shape
    prompt_len = prompt_pool.shape[2]
    chans = width // sections
    tap_len, group_all = long_taps.shape[1:]
    per_group = width // group_all
    dims = (sections, n_resp, micro, length, prompt_len, chans, per_group, width)

    tiles = 2 * chans // LANES
    direct = n_resp <= 8 and tiles % n_resp == 0

    gs = jnp.concatenate([norm_gain, short_taps[0]], axis=0)
    taps = long_taps[0].T
    flipped = jnp.concatenate([taps[:, :1], taps[:, :0:-1]], axis=1)
    taps = jnp.concatenate([flipped, taps], axis=1)
    prompts = prompt_pool[0, 0]
    mine = prompt_owner[:, None] == jnp.arange(n_resp, dtype=jnp.int32)[None]
    chosen = jnp.broadcast_to(
        mine.astype(F32).reshape(micro * n_resp, 1), (micro * n_resp, LANES)
    )
    if not direct:
        split = prompts.reshape(prompt_len, sections, chans).transpose(1, 0, 2)
        split = lax.all_to_all(split, "section", 0, 0, tiled=True)
        here = (prompt_owner == me_resp)[None, :, None, None]
        split = lax.psum(jnp.where(here, split[:, None], jnp.zeros((), BF16)), "resp")
        prompts = split.reshape(sections, micro * prompt_len, chans)
    rows = completion_rows.reshape(micro * length, width)
    head = score_head[None]

    labels = jnp.arange(n_resp, dtype=jnp.int32)[:, None, None]
    ends = (pair_index[None, :, :, 0] == labels).astype(F32) - (
        pair_index[None, :, :, 1] == labels
    ).astype(F32)
    pairs = jnp.pad(ends, ((0, 0), (0, 8 - micro), (0, LANES - ends.shape[2])))
    own_pairs = lax.dynamic_index_in_dim(pairs, me_resp, 0, keepdims=False)
    lengths = live_lengths[:, 0]
    live = (jnp.arange(length, dtype=jnp.int32)[None] < lengths[:, None]).astype(F32)
    live = (live / jnp.sqrt(lengths.astype(F32))[:, None]).reshape(micro * length, 1)
    live = jnp.broadcast_to(live, (micro * length, LANES))

    scores, grads = run_kernel(
        dims, direct, rows, prompts, gs, taps, chosen, head, pairs, own_pairs, live
    )
    if not direct:
        grads = lax.psum(grads, "resp")
        grads = lax.all_to_all(grads, "section", 0, 0, tiled=True)
    grads = grads.reshape(sections * tiles // 2, 2, 8, LANES)
    gs_grad = grads[:, 0].transpose(1, 0, 2).reshape(8, width)
    taps_grad = grads[:, 1].reshape(group_all, tap_len).T
    return (
        scores[:micro, :1].astype(BF16),
        gs_grad[:1],
        gs_grad[None, 1:],
        taps_grad[None],
    )


def solution(mesh):
    placed = (
        P(None, ("groups", "resp"), None, None),
        P("section", ("groups", "resp"), None, None),
        P("section", None),
        P("section", None, None),
        P("section", None, None),
        P(),
        P(None, ("groups", "resp")),
        P("groups"),
        P(None, "groups", None),
    )
    return jax.shard_map(
        body,
        mesh=mesh,
        in_specs=placed,
        out_specs=(
            P(None, ("groups", "resp")),
            P("section", "groups"),
            P("section", "groups", None),
            P("section", "groups", None),
        ),
        check_vma=False,
    )
```

time: 1090 us -> 180 us (0.17)
  waiting for transfers between devices: 477 us -> 0 us
  Pallas kernels: 0 us -> 165 us
  other arithmetic: 157 us -> 4.37 us
  matrix products: 151 us -> 0 us
  local copies, waits for them, and re-layouts: 148 us -> 8.37 us
  starting transfers between devices: 68.4 us -> 0 us
  loops' own time: 34.5 us -> 0 us
  blocking collectives: 25.6 us -> 0 us
  between operations: 24.9 us -> 0.69 us
    ppermute x12 -> x0, waiting for transfers between devices: 368 us -> none  [from_behind(): return lax.ppermute(block, axis, route)]
    pallas_call x0 -> x1, Pallas kernels: none -> 165 us  [run_kernel(): pl.pallas_call(functools.partial(kernel, dims, direct), out_shape=(jax.Sh...]
    dot_general x15 -> x0, matrix products: 151 us -> none  [the longest x8 120 us: filters_apply(): jnp.einsum('gts,sgk->tgk', toep, grouped, precision=lax.Precision.HIGHEST)]
    psum x2 -> x0, waiting for transfers between devices: 109 us -> none  [the longest x1 94 us: spread(): return lax.psum(jnp.where(mine, value, jnp.zeros_like(value)), axis)]
    ppermute x12 -> x0, starting transfers between devices: 68.4 us -> none  [from_behind(): return lax.ppermute(block, axis, route)]
    another operation x32 -> x0, local copies, waits for them, and re-layouts: 67.1 us -> none
    add x8 -> x0, other arithmetic: 54.3 us -> none  [the longest x4 33.5 us: filters_apply(): shorter + short_row[offset][None, :] * padded[begin:begin + count_rows]]
    reduce_sum x10 -> x0, other arithmetic: 39.8 us -> none  [the longest x2 24 us: filters_apply(): short_row[offset][None, :] * padded[begin:begin + count_rows]]
  transfers between devices with their start and end apart: 14 -> 0, of which waited for: 7 -> 0; matrix products, arithmetic and copies ran while one was open for 27% -> 0% of each run, Pallas kernels for 0% -> 0%
where the time goes in v1:
time: 180 us; the launch traced here: 179 us
  Pallas kernels  165 us (92%)
  local copies, waits for them, and re-layouts  8.37 us (5%)
  other arithmetic  4.37 us (2%)
    pallas_call x1, Pallas kernels, run_kernel(): pl.pallas_call(functools.partial(kernel, dims, direct), out_shape=(jax.Sh...  165 us

profile of v1, /device:TPU:0, one launch (start us, length us, event | category | flops | bytes accessed | tf_op | source)
XLA Modules:
  0.0 178.7 jit_solution(3909979317350108491)
XLA Ops:
  0.6 0.0 copy-start.1
  0.6 0.7 sqrt_bitcast_fusion
  1.3 0.7 fusion.2
  2.1 0.1 div.20
  2.2 0.7 compare_convert_fusion.3
  2.9 0.1 reshape.66
  3.0 0.8 fusion.3
  3.7 0.6 fusion.own_pairs_ref
  4.3 0.6 broadcast_in_dim.10.chosen_ref
  5.0 0.6 pad.4.pairs_ref
  5.6 0.7 broadcast_in_dim.12.live_ref
  6.3 0.0 copy-done.1
  6.3 0.0 copy-start.2
  6.3 0.1 copy.23
  6.4 0.6 copy-done.2
  7.0 0.0 copy-start
  7.0 0.7 pad_maximum_fusion.1.gs_hbm
  7.7 0.2 copy-done
  8.0 0.1 copy.16
  8.1 0.1 slice.43
  8.2 0.2 rev.3
  8.3 0.9 pad_maximum_fusion.taps_hbm
  9.2 165.3 %shard_map.120 = (f32[8,128]{1,0:T(8,128)}, f32[4,4,4,8,128]{4,3,2,1,0:T(8,128)}) custom-call(bf16[128,4096]{1,0:T(8,128)(2,1)} %bitcast.36, bf16[64,4096]{1,0:T(8,128)(2,1)} %bitcast.38, f32[8,4096]{1,0:T(8,128)} %pad_maximum_fusion.1.gs_hbm, f32[256,256]{1,0:T(8,128)} %pad_maximum_fusion.taps_hbm, f32[8,128]{1,0:T(8,128)} %broadcast_in_dim.10.chosen_ref, ...), custom_call_target="tpu_custom_call" | custom-call | tf_op jit(solution)/shard_map/pallas_call | solution.py:560
  174.5 0.7 convert.4
  175.2 0.5 slice.36
  175.7 1.0 slice_bitcast_fusion
  176.7 0.8 copy.19
  177.4 0.6 slice_bitcast_fusion.2
  178.1 0.7 copy.17
  (2 shorter events, 0.0 us)
Async XLA Ops:
  0.6 5.7 %copy-start.1 = (f32[1,7,4096]{2,0,1:T(1,128)S(1)}, f32[1,7,4096]{2,0,1:T(1,128)}, u32[]{:S(2)}) copy-start(f32[1,7,4096]{2,0,1:T(1,128)} %param.12) | copy-start | bytes 344068
  6.3 0.7 copy-start.2
  7.0 0.9 copy-start

commit v2 on v1

--- a/solution.py
+++ b/solution.py
@@ -27,49 +27,54 @@
     direct,
     comp_ref,
     prompt_ref,
-    gs_hbm,
+    gain_hbm,
+    short_hbm,
     taps_hbm,
-    chosen_ref,
+    owner_ref,
     head_ref,
-    pairs_ref,
-    own_pairs_ref,
-    live_ref,
+    ends_ref,
+    length_ref,
     score_ref,
-    tiles_ref,
-    toep,
-    toep_t,
-    pool,
-    chosen_rows,
-    gs_ref,
-    taps_ref,
-    rows_in,
-    short_out,
-    long_out,
-    fac_p,
-    fac_c,
-    upstream,
-    partial,
-    stat_acc,
-    score_acc,
-    prompt_acc,
-    stat_out,
-    stat_in,
-    resp_out,
-    resp_in,
-    tiles_own,
-    tiles_in,
-    tiles_sum,
-    local_sem,
-    weight_sems,
-    pool_send,
-    pool_recv,
-    stat_sems,
-    resp_sems,
-    part_sems,
-    tile_send,
-    tile_recv,
+    *rest,
 ):
     sections, n_resp, micro, length, prompt_len, chans, per_group, width = dims
+    outs, rest = (rest[:3], rest[3:]) if direct else (rest[:1], rest[1:])
+    (
+        toep,
+        toep_t,
+        pool,
+        chosen_rows,
+        gain_ref,
+        short_ref,
+        taps_ref,
+        rows_in,
+        short_out,
+        long_out,
+        fac_p,
+        fac_c,
+        upstream,
+        partial,
+        stat_acc,
+        score_acc,
+        prompt_acc,
+        stat_out,
+        stat_in,
+        resp_out,
+        resp_in,
+        tiles_own,
+        tiles_in,
+        tiles_sum,
+        tiles_all,
+        local_sem,
+        weight_sems,
+        spread_sems,
+        pool_sems,
+        stat_sems,
+        resp_sems,
+        part_sems,
+        tile_send,
+        tile_recv,
+    ) = rest
     groups = LANES // per_group
     blocks = chans // LANES
     group_rows = blocks * groups
@@ -136,7 +141,8 @@
                 device_id_type=MESH,
             )
             for kind, source, target in (
-                (0, gs_hbm.at[:, lanes], gs_ref.at[me]),
+                (0, gain_hbm.at[:, lanes], gain_ref.at[me]),
+                (2, short_hbm.at[:, lanes], short_ref.at[me]),
                 (1, taps_hbm.at[rows, :], taps_ref.at[me]),
             )
         ]
@@ -152,68 +158,57 @@
     own_rows = pl.ds(pl.multiple_of(me * group_rows, group_rows), group_rows)
     local_copies = [
         pltpu.make_async_copy(comp_ref.at[:, own_lanes], rows_in.at[0], local_sem.at[0]),
-        pltpu.make_async_copy(gs_hbm.at[:, own_lanes], gs_ref.at[me], local_sem.at[1]),
+        pltpu.make_async_copy(gain_hbm.at[:, own_lanes], gain_ref.at[me], local_sem.at[1]),
+        pltpu.make_async_copy(short_hbm.at[:, own_lanes], short_ref.at[me], local_sem.at[3]),
         pltpu.make_async_copy(taps_hbm.at[own_rows, :], taps_ref.at[me], local_sem.at[2]),
     ]
 
-    def pool_copy(section_step, resp_step):
-        peer = lax.rem(me + section_step, sections)
+    def spread_copy(step):
+        peer = lax.rem(me + step, sections)
         lanes = pl.ds(pl.multiple_of(peer * chans, chans), chans)
         return pltpu.make_async_remote_copy(
             src_ref=prompt_ref.at[:, lanes],
             dst_ref=pool.at[me, me_resp],
-            send_sem=pool_send.at[section_step, resp_step],
-            recv_sem=pool_recv.at[me, me_resp],
-            device_id={"section": peer, "resp": lax.rem(me_resp + resp_step, n_resp)},
+            send_sem=spread_sems.at[0, step],
+            recv_sem=spread_sems.at[1, step],
+            device_id={"section": peer},
             device_id_type=MESH,
         )
 
-    def pool_arrival(s, r):
+    def pool_copy(s, step):
         return pltpu.make_async_remote_copy(
-            src_ref=prompt_ref.at[:, own_lanes],
-            dst_ref=pool.at[s, r],
-            send_sem=pool_send.at[0, 0],
-            recv_sem=pool_recv.at[s, r],
-            device_id={"section": lax.rem(me + 1, sections)},
+            src_ref=pool.at[s, me_resp],
+            dst_ref=pool.at[s, me_resp],
+            send_sem=pool_sems.at[0, s, step],
+            recv_sem=pool_sems.at[1, s, step],
+            device_id={"resp": lax.rem(me_resp + step, n_resp)},
             device_id_type=MESH,
         )
 
-    own_pool = (
-        pltpu.make_async_copy(
-            prompt_ref.at[:, own_lanes], pool.at[me, me_resp], pool_recv.at[me, me_resp]
+    def own_pool():
+        return pltpu.make_async_copy(
+            prompt_ref.at[:, own_lanes], pool.at[me, me_resp], local_sem.at[4]
         )
-        if direct
-        else None
-    )
-
-    def pool_steps(action):
-        def each(step):
-            @pl.when(step > 0)
-            def _():
-                action(pool_copy(step // n_resp, step % n_resp))
-
-        loop(0, sections * n_resp, each)
 
     def start_pool(s):
-        @pl.when(me == s)
+        step = lax.rem(me - s + sections, sections)
+
+        @pl.when(step == 0)
         def _():
-            own_pool.start()
-            pool_steps(lambda copy: copy.start())
+            own_pool().wait()
+
+        @pl.when(step > 0)
+        def _():
+            spread_copy(step).wait()
+
+        loop(1, n_resp, lambda d: pool_copy(s, d).start())
 
     def wait_pool(s):
-        def each(r):
-            mine = (s == me) & (r == me_resp)
-
-            @pl.when(mine)
-            def _():
-                own_pool.wait()
-
-            @pl.when(jnp.logical_not(mine))
-            def _():
-                pool_arrival(s, r).wait_recv()
-
-        loop(0, n_resp, each)
-
+        loop(1, n_resp, lambda d: pool_copy(s, d).wait())
+
+    if direct:
+        own_pool().start()
+        loop(1, sections, lambda step: spread_copy(step).start())
     for copy in local_copies:
         copy.start()
     loop(1, sections, start_weights)
@@ -261,7 +256,7 @@
             if direct:
                 picked = jnp.zeros((prompt_len, LANES), F32)
                 for r in range(n_resp):
-                    flag = chosen_ref[m * n_resp + r : m * n_resp + r + 1, :] > 0.5
+                    flag = jnp.full((prompt_len, LANES), owner_ref[m], jnp.int32) == r
                     picked = jnp.where(flag, pool[s, r, :, lanes].astype(F32), picked)
                 chosen_rows[s, rows, lanes] = picked.astype(BF16)
             else:
@@ -273,7 +268,7 @@
     wide_group = (
         lax.broadcasted_iota(jnp.int32, (1, micro * LANES), 1) % LANES
     ) // per_group
-    tap_count = gs_ref.shape[1] - 1
+    tap_count = short_ref.shape[1]
 
     def pick(stacked, rows):
         out = stacked[0:rows]
@@ -294,7 +289,11 @@
     def forward(s, carry):
         if direct:
             wait_pool(s)
-            start_pool(s + 1)
+
+            @pl.when(s + 1 < sections)
+            def _():
+                start_pool(s + 1)
+
         prompt_acc[...] = jnp.zeros_like(prompt_acc)
         loop(0, blocks, lambda block: choose(s, block))
         finish = start_stats(s, rows_to_line(stat_acc[...]), rows_to_line(prompt_acc[...]))
@@ -308,15 +307,16 @@
         def run(block, carry):
             lanes = lane_slice(block)
             wide = wide_slice(block)
-            gs = gs_ref[s, :, lanes]
+            gain = gain_ref[s, :, lanes]
+            short = short_ref[s, :, lanes]
             parts, lows, saved = [], [], []
             for m in range(micro):
                 joined, factor = joined_rows(s, m, lanes)
-                normed = joined * factor * gs[0:1]
-                shorter = normed * gs[1:2]
+                normed = joined * factor * gain
+                shorter = normed * short[0:1]
                 for j in range(1, tap_count):
                     moved = jnp.where(row_id >= j, pltpu.roll(normed, j, 0), 0.0)
-                    shorter = shorter + moved * gs[1 + j : 2 + j]
+                    shorter = shorter + moved * short[j : j + 1]
                 high = shorter.astype(BF16)
                 parts.append(high)
                 lows.append((shorter - high.astype(F32)).astype(BF16))
@@ -346,10 +346,14 @@
 
     lax.fori_loop(0, sections, forward, 0)
 
+    live = []
+    for m in range(micro):
+        count = jnp.full((length, LANES), length_ref[m, 0], jnp.int32)
+        live.append(jnp.where(t_row < count, 1.0, 0.0) / jnp.sqrt(count.astype(F32)))
     tile_rows = []
     for m in range(micro):
         rows = slice(m * length, (m + 1) * length)
-        line = jnp.sum(score_acc[rows, :] * live_ref[rows, :], axis=0, keepdims=True)
+        line = jnp.sum(score_acc[rows, :] * live[m], axis=0, keepdims=True)
         tile_rows.append(jnp.broadcast_to(jnp.sum(line, axis=1, keepdims=True), (1, LANES)))
     tile_rows.append(jnp.zeros((8 - micro, LANES), F32))
     score_tile = jnp.concatenate(tile_rows, axis=0)
@@ -357,15 +361,22 @@
     score_ref[...] = own_score
     resp_out[...] = own_score
     swap("resp", n_resp, me_resp, resp_out, resp_in, resp_sems)()
-    margin = jnp.sum(resp_in[...] * pairs_ref[...], axis=0)
+    winner, loser = ends_ref[0], ends_ref[1]
+
+    def signs(r):
+        return jnp.where(winner == r, 1.0, 0.0) - jnp.where(loser == r, 1.0, 0.0)
+
+    margin = lax.fori_loop(
+        0, n_resp, lambda r, acc: acc + resp_in[r] * signs(r), jnp.zeros((8, LANES), F32)
+    )
     weight = 1.0 / (1.0 + jnp.exp(margin))
-    slopes = -jnp.sum(own_pairs_ref[...] * weight, axis=1, keepdims=True)
+    slopes = -jnp.sum(signs(me_resp) * weight, axis=1, keepdims=True)
 
     def seed(block, carry):
         lanes = lane_slice(block)
         for m in range(micro):
             rows = slice(m * length, (m + 1) * length)
-            upstream[rows, lanes] = live_ref[rows, :] * slopes[m : m + 1] * head_ref[0:1, head_slice(block)]
+            upstream[rows, lanes] = live[m] * slopes[m : m + 1] * head_ref[0:1, head_slice(block)]
         return carry
 
     lax.fori_loop(0, blocks, seed, 0)
@@ -402,7 +413,7 @@
     def tile_copy(s, step, k, r):
         return pltpu.make_async_remote_copy(
             src_ref=tiles_sum.at[s],
-            dst_ref=tiles_ref.at[k, r],
+            dst_ref=tiles_all.at[k, r],
             send_sem=tile_send.at[s, step],
             recv_sem=tile_recv.at[k, r],
             device_id={"section": s, "resp": lax.rem(me_resp + step, n_resp)},
@@ -424,13 +435,14 @@
         def run(block, carry):
             lanes = lane_slice(block)
             wide = wide_slice(block)
-            gs = gs_ref[s, :, lanes]
+            gain = gain_ref[s, :, lanes]
+            short = short_ref[s, :, lanes]
             parts, saved = [], []
             for m in range(micro):
                 rows = slice(m * length, (m + 1) * length)
                 joined, factor = joined_rows(s, m, lanes)
                 scaled = joined * factor
-                normed = scaled * gs[0:1]
+                normed = scaled * gain
                 above = upstream[rows, lanes]
                 parts.append((above * normed[prompt_len:]).astype(BF16))
                 saved.append((joined[prompt_len:], scaled, normed, above))
@@ -468,13 +480,13 @@
                 rows = slice(m * length, (m + 1) * length)
                 joined_c, scaled, normed, above = saved[m]
                 d_short = d_short_all[:, m * LANES : (m + 1) * LANES]
-                d_normed = d_short * gs[1:2]
+                d_normed = d_short * short[0:1]
                 grads[1] = grads[1] + jnp.sum(d_short * normed, axis=0, keepdims=True)
                 for j in range(1, tap_count):
                     moved = jnp.where(
                         row_id < total - j, pltpu.roll(d_short, total - j, 0), 0.0
                     )
-                    d_normed = d_normed + moved * gs[1 + j : 2 + j]
+                    d_normed = d_normed + moved * short[j : j + 1]
                     grads[1 + j] = grads[1 + j] + jnp.sum(
                         moved * normed, axis=0, keepdims=True
                     )
@@ -483,7 +495,7 @@
                     [d_normed[:prompt_len], d_normed[prompt_len:] + direct], axis=0
                 )
                 grads[0] = grads[0] + jnp.sum(d_normed * scaled, axis=0, keepdims=True)
-                inner = d_normed[prompt_len:] * gs[0:1]
+                inner = d_normed[prompt_len:] * gain
                 partial[rows, lanes] = inner
                 stat_acc[rows, :] += inner * joined_c
             tiles_own[s, 2 * block] = jnp.concatenate(grads, axis=0)
@@ -521,7 +533,7 @@
 
             @pl.when(s == me)
             def _():
-                tiles_ref[me, me_resp] = tiles_sum[s]
+                tiles_all[me, me_resp] = tiles_sum[s]
 
             tile_steps(s, lambda copy: copy.start())
 
@@ -530,7 +542,6 @@
     lax.fori_loop(0, sections, backward, 0)
 
     if direct:
-        pool_steps(lambda copy: copy.wait_send())
         loop(0, sections, lambda s: tile_steps(s, lambda copy: copy.wait_send()))
 
         def arrive(step):
@@ -541,8 +552,23 @@
                 tile_copy(0, 0, k, r).wait_recv()
 
         loop(0, sections * n_resp, arrive)
+        gain_out, taps_short_out, taps_long_out = outs
+        per_line = LANES // groups
+        for line in range(sections * blocks // per_line):
+            lines = []
+            for place in range(per_line):
+                block = line * per_line + place
+                lanes = slice(block * LANES, (block + 1) * LANES)
+                owner, local = divmod(2 * block, 2 * blocks)
+                first, second = (divmod(local + kind, share) for kind in range(2))
+                tile = tiles_all[owner, first[0], first[1]]
+                gain_out[:, lanes] = tile[0:1]
+                taps_short_out[:, lanes] = tile[1:]
+                lines.append(tiles_all[owner, second[0], second[1]])
+            lanes = slice(line * LANES, (line + 1) * LANES)
+            taps_long_out[:, lanes] = jnp.transpose(jnp.concatenate(lines, axis=0))
     else:
-        tiles_ref[...] = tiles_own[...]
+        outs[0][...] = tiles_own[...]
 
 
 def run_kernel(dims, direct, *arrays):
@@ -556,21 +582,27 @@
     ranks = n_resp if direct else 1
     vmem = pl.BlockSpec(memory_space=pltpu.VMEM)
     hbm = pl.BlockSpec(memory_space=pl.ANY)
-    tiles_shape = (sections, n_resp, share) if direct else (sections, tiles)
+    smem = pl.BlockSpec(memory_space=pltpu.SMEM)
+    tap_count = arrays[3].shape[0]
+    if direct:
+        out_shapes = [(1, width), (tap_count, width), (LANES, width // per_group)]
+    else:
+        out_shapes = [(sections, tiles) + tile]
     return pl.pallas_call(
         functools.partial(kernel, dims, direct),
         out_shape=(
             jax.ShapeDtypeStruct(tile, F32),
-            jax.ShapeDtypeStruct(tiles_shape + tile, F32),
+            *(jax.ShapeDtypeStruct(shape, F32) for shape in out_shapes),
         ),
-        in_specs=[hbm, hbm if direct else vmem, hbm, hbm] + [vmem] * (len(arrays) - 4),
-        out_specs=(vmem,) * 2,
+        in_specs=[hbm, hbm if direct else vmem, hbm, hbm, hbm, smem, vmem, vmem, smem],
+        out_specs=(vmem,) * (1 + len(out_shapes)),
         scratch_shapes=[
             pltpu.VMEM((sections, group_total * length, 3 * LANES), BF16),
             pltpu.VMEM((sections, group_total * total, LANES), BF16),
             pltpu.VMEM((sections, ranks, prompt_len, chans), BF16),
             pltpu.VMEM((sections, micro * prompt_len, chans), BF16),
-            pltpu.VMEM((sections, 8, chans), F32),
+            pltpu.VMEM((sections, 1, chans), F32),
+            pltpu.VMEM((sections, tap_count, chans), F32),
             pltpu.VMEM((sections, group_total, 2 * LANES), F32),
             pltpu.VMEM((sections + 1, rows, chans), BF16),
             pltpu.VMEM((sections, total, micro * chans), BF16),
@@ -589,10 +621,11 @@
             pltpu.VMEM((sections, tiles) + tile, F32),
             pltpu.VMEM((sections, ranks, share) + tile, F32),
             pltpu.VMEM((sections, share) + tile, F32),
-            pltpu.SemaphoreType.DMA((3,)),
-            pltpu.SemaphoreType.DMA((2, 2, sections)),
-            pltpu.SemaphoreType.DMA((sections, ranks)),
-            pltpu.SemaphoreType.DMA((sections, ranks)),
+            pltpu.VMEM((sections, ranks, share) + tile, F32),
+            pltpu.SemaphoreType.DMA((5,)),
+            pltpu.SemaphoreType.DMA((2, 3, sections)),
+            pltpu.SemaphoreType.DMA((2, sections)),
+            pltpu.SemaphoreType.DMA((2, sections, ranks)),
             pltpu.SemaphoreType.DMA((2 * sections, 2, sections)),
             pltpu.SemaphoreType.DMA((2, n_resp)),
             pltpu.SemaphoreType.DMA((2, sections, ranks)),
@@ -629,15 +662,10 @@
     tiles = 2 * chans // LANES
     direct = n_resp <= 8 and tiles % n_resp == 0
 
-    gs = jnp.concatenate([norm_gain, short_taps[0]], axis=0)
     taps = long_taps[0].T
     flipped = jnp.concatenate([taps[:, :1], taps[:, :0:-1]], axis=1)
     taps = jnp.concatenate([flipped, taps], axis=1)
     prompts = prompt_pool[0, 0]
-    mine = prompt_owner[:, None] == jnp.arange(n_resp, dtype=jnp.int32)[None]
-    chosen = jnp.broadcast_to(
-        mine.astype(F32).reshape(micro * n_resp, 1), (micro * n_resp, LANES)
-    )
     if not direct:
         split = prompts.reshape(prompt_len, sections, chans).transpose(1, 0, 2)
         split = lax.all_to_all(split, "section", 0, 0, tiled=True)
@@ -647,28 +675,34 @@
     rows = completion_rows.reshape(micro * length, width)
     head = score_head[None]
 
-    labels = jnp.arange(n_resp, dtype=jnp.int32)[:, None, None]
-    ends = (pair_index[None, :, :, 0] == labels).astype(F32) - (
-        pair_index[None, :, :, 1] == labels
-    ).astype(F32)
-    pairs = jnp.pad(ends, ((0, 0), (0, 8 - micro), (0, LANES - ends.shape[2])))
-    own_pairs = lax.dynamic_index_in_dim(pairs, me_resp, 0, keepdims=False)
-    lengths = live_lengths[:, 0]
-    live = (jnp.arange(length, dtype=jnp.int32)[None] < lengths[:, None]).astype(F32)
-    live = (live / jnp.sqrt(lengths.astype(F32))[:, None]).reshape(micro * length, 1)
-    live = jnp.broadcast_to(live, (micro * length, LANES))
-
-    scores, grads = run_kernel(
-        dims, direct, rows, prompts, gs, taps, chosen, head, pairs, own_pairs, live
+    ends = jnp.pad(
+        pair_index.transpose(2, 0, 1),
+        ((0, 0), (0, 8 - micro), (0, LANES - pair_index.shape[1])),
+        constant_values=-1,
     )
-    if not direct:
-        grads = lax.psum(grads, "resp")
-        grads = lax.all_to_all(grads, "section", 0, 0, tiled=True)
+    scores, *grads = run_kernel(
+        dims,
+        direct,
+        rows,
+        prompts,
+        norm_gain,
+        short_taps[0],
+        taps,
+        prompt_owner,
+        head,
+        ends,
+        live_lengths,
+    )
+    scores = scores[:micro, :1].astype(BF16)
+    if direct:
+        return (scores, grads[0], grads[1][None], grads[2][None])
+    grads = lax.psum(grads[0], "resp")
+    grads = lax.all_to_all(grads, "section", 0, 0, tiled=True)
     grads = grads.reshape(sections * tiles // 2, 2, 8, LANES)
     gs_grad = grads[:, 0].transpose(1, 0, 2).reshape(8, width)
     taps_grad = grads[:, 1].reshape(group_all, tap_len).T
     return (
-        scores[:micro, :1].astype(BF16),
+        scores,
         gs_grad[:1],
         gs_grad[None, 1:],
         taps_grad[None],

time: 180 us -> 132 us (0.73)
  Pallas kernels: 165 us -> 123 us
  other arithmetic: 4.37 us -> 0.86 us
    pallas_call x1, Pallas kernels: 165 us -> 123 us  [run_kernel(): pl.pallas_call(functools.partial(kernel, dims, direct), out_shape=(jax.Sh...]
    unnamed x9 -> x19, local copies, waits for them, and re-layouts: 1.8 us -> 6.63 us
    broadcast_in_dim x3 -> x0, local copies, waits for them, and re-layouts: 2.34 us -> none  [the longest x1 0.99 us: body(): taps_grad[None]]
    slice x5 -> x1, local copies, waits for them, and re-layouts: 2.57 us -> 0.51 us  [body(): scores = scores[:micro, :1].astype(BF16)]
where the time goes in v2:
time: 132 us
  Pallas kernels  123 us (93%)
  local copies, waits for them, and re-layouts  8.03 us (6%)
    pallas_call x1, Pallas kernels, run_kernel(): pl.pallas_call(functools.partial(kernel, dims, direct), out_shape=(jax.Sh...  123 us
    unnamed x19, local copies, waits for them, and re-layouts  6.63 us

profile of v2, /device:TPU:0, one launch (start us, length us, event | category | flops | bytes accessed | tf_op | source)
XLA Modules:
  0.0 132.2 jit_solution(15648880753433384727)
XLA Ops:
  0.6 0.0 copy-start.5
  0.6 0.0 copy-start.4
  0.7 0.6 copy-done.5
  1.3 0.6 copy.15.length_ref
  1.9 0.0 copy-done.4
  1.9 0.0 copy-start
  1.9 0.6 pad.4.ends_ref
  2.5 1.6 %copy.20 = f32[1,7,4096]{2,1,0:T(8,128)} copy(f32[1,7,4096]{2,0,1:T(1,128)} %param.12) | data formatting | bytes 229376
  4.2 0.0 copy-done
  4.2 0.1 copy.13
  4.3 0.1 slice.14
  4.4 0.2 rev.3
  4.6 0.9 pad_maximum_fusion.taps_hbm
  5.4 122.6 %shard_map.120 = (f32[8,128]{1,0:T(8,128)}, f32[1,4096]{1,0:T(1,128)}, f32[7,4096]{1,0:T(8,128)}, f32[128,256]{1,0:T(8,128)}) custom-call(bf16[128,4096]{1,0:T(8,128)(2,1)} %bitcast.18, bf16[64,4096]{1,0:T(8,128)(2,1)} %bitcast.20, f32[1,4096]{1,0:T(1,128)} %gain_hbm.1, f32[7,4096]{1,0:T(8,128)} %bitcast.19, f32[256,256]{1,0:T(8,128)} %pad_maximum_fusion.taps_hbm, ...), custom_call_target="tpu_custom_call" | custom-call | tf_op jit(solution)/shard_map/pallas_call | solution.py:591
  128.0 0.0 copy-start.3
  128.1 0.7 copy-done.3
  128.7 0.5 slice.12
  129.2 0.0 copy-start.2
  129.2 0.0 copy-start.1
  129.2 1.7 %copy.16 = f32[1,7,4096]{2,0,1:T(1,128)} copy(f32[1,7,4096]{2,1,0:T(8,128)} %bitcast.22) | data formatting | bytes 229376
  130.9 0.0 copy-done.2
  130.9 0.6 copy.24
  131.5 0.0 copy-done.1
  131.5 0.7 copy.25
  (2 shorter events, 0.0 us)
Async XLA Ops:
  0.6 0.7 copy-start.5
  0.6 1.3 copy-start.4
  1.9 2.2 %copy-start = (f32[1,128,256]{2,1,0:T(8,128)S(1)}, f32[1,128,256]{2,1,0:T(8,128)}, u32[]{:S(2)}) copy-start(f32[1,128,256]{2,1,0:T(8,128)} %param.13) | copy-start | bytes 393220
  128.0 0.7 copy-start.3
  129.2 1.7 %copy-start.2 = (f32[1,4096]{1,0:T(1,128)S(1)}, f32[1,4096]{1,0:T(1,128)}, u32[]{:S(2)}) copy-start(f32[1,4096]{1,0:T(1,128)} %get-tuple-element.21) | copy-start | bytes 49156
  129.2 2.3 %copy-start.1 = (f32[128,256]{1,0:T(8,128)S(1)}, f32[128,256]{1,0:T(8,128)}, u32[]{:S(2)}) copy-start(f32[128,256]{1,0:T(8,128)} %get-tuple-element.11) | copy-start | bytes 393220

commit v3 on v2

--- a/solution.py
+++ b/solution.py
@@ -142,7 +142,7 @@
             )
             for kind, source, target in (
                 (0, gain_hbm.at[:, lanes], gain_ref.at[me]),
-                (2, short_hbm.at[:, lanes], short_ref.at[me]),
+                (2, short_hbm.at[:, :, lanes], short_ref.at[me]),
                 (1, taps_hbm.at[rows, :], taps_ref.at[me]),
             )
         ]
@@ -159,7 +159,7 @@
     local_copies = [
         pltpu.make_async_copy(comp_ref.at[:, own_lanes], rows_in.at[0], local_sem.at[0]),
         pltpu.make_async_copy(gain_hbm.at[:, own_lanes], gain_ref.at[me], local_sem.at[1]),
-        pltpu.make_async_copy(short_hbm.at[:, own_lanes], short_ref.at[me], local_sem.at[3]),
+        pltpu.make_async_copy(short_hbm.at[:, :, own_lanes], short_ref.at[me], local_sem.at[3]),
         pltpu.make_async_copy(taps_hbm.at[own_rows, :], taps_ref.at[me], local_sem.at[2]),
     ]
 
@@ -206,12 +206,12 @@
     def wait_pool(s):
         loop(1, n_resp, lambda d: pool_copy(s, d).wait())
 
+    loop(1, sections, start_weights)
     if direct:
         own_pool().start()
         loop(1, sections, lambda step: spread_copy(step).start())
     for copy in local_copies:
         copy.start()
-    loop(1, sections, start_weights)
     if direct:
         start_pool(0)
     for copy in local_copies:
@@ -232,10 +232,10 @@
     t_lane = lax.broadcasted_iota(jnp.int32, (total, LANES), 1)
     keep_t = s_row <= prompt_len + t_lane
 
-    def build(s, block):
+    def build(step):
+        s, block = step // blocks, step % blocks
         rows = pl.ds(pl.multiple_of(block * groups, groups), groups)
-        both = taps_ref[s, rows, :]
-        flipped, plain = both[:, :LANES], both[:, LANES:]
+        flipped = taps_ref[s, rows, :][:, :LANES]
         for g in range(groups):
             base = pl.multiple_of((block * groups + g) * length, length)
             wide = jnp.broadcast_to(flipped[g : g + 1], (length, LANES))
@@ -244,10 +244,17 @@
             high = wide.astype(BF16)
             low = (wide - high.astype(F32)).astype(BF16)
             toep[s, pl.ds(base, length), :] = jnp.concatenate([high, high, low], axis=1)
+
+    def build_t(s, block):
+        rows = pl.ds(pl.multiple_of(block * groups, groups), groups)
+        plain = taps_ref[s, rows, :][:, LANES:]
+        for g in range(groups):
             base = pl.multiple_of((block * groups + g) * total, total)
             wide = jnp.broadcast_to(plain[g : g + 1], (total, LANES))
             wide = pltpu.roll(wide, prompt_len, 1, stride=1, stride_axis=0)
             toep_t[s, pl.ds(base, total), :] = jnp.where(keep_t, wide, 0.0).astype(BF16)
+
+    loop(0, sections * blocks, build)
 
     def choose(s, block):
         lanes = lane_slice(block)
@@ -268,7 +275,7 @@
     wide_group = (
         lax.broadcasted_iota(jnp.int32, (1, micro * LANES), 1) % LANES
     ) // per_group
-    tap_count = short_ref.shape[1]
+    tap_count = short_hbm.shape[0]
 
     def pick(stacked, rows):
         out = stacked[0:rows]
@@ -297,7 +304,7 @@
         prompt_acc[...] = jnp.zeros_like(prompt_acc)
         loop(0, blocks, lambda block: choose(s, block))
         finish = start_stats(s, rows_to_line(stat_acc[...]), rows_to_line(prompt_acc[...]))
-        loop(0, blocks, lambda block: build(s, block))
+        loop(0, blocks, lambda block: build_t(s, block))
         sums = finish()
         fac_c[s] = lax.rsqrt(line_to_rows(sums[0]) * (1.0 / width) + 1e-06)
         fac_p[s] = lax.rsqrt(line_to_rows(sums[1]) * (1.0 / width) + 1e-06)
@@ -308,7 +315,9 @@
             lanes = lane_slice(block)
             wide = wide_slice(block)
             gain = gain_ref[s, :, lanes]
-            short = short_ref[s, :, lanes]
+            short = jnp.concatenate(
+                [short_ref[s, j, :, lanes] for j in range(tap_count)], axis=0
+            )
             parts, lows, saved = [], [], []
             for m in range(micro):
                 joined, factor = joined_rows(s, m, lanes)
@@ -436,7 +445,9 @@
             lanes = lane_slice(block)
             wide = wide_slice(block)
             gain = gain_ref[s, :, lanes]
-            short = short_ref[s, :, lanes]
+            short = jnp.concatenate(
+                [short_ref[s, j, :, lanes] for j in range(tap_count)], axis=0
+            )
             parts, saved = [], []
             for m in range(micro):
                 rows = slice(m * length, (m + 1) * length)
@@ -563,10 +574,11 @@
                 first, second = (divmod(local + kind, share) for kind in range(2))
                 tile = tiles_all[owner, first[0], first[1]]
                 gain_out[:, lanes] = tile[0:1]
-                taps_short_out[:, lanes] = tile[1:]
+                for j in range(tap_count):
+                    taps_short_out[j, :, lanes] = tile[1 + j : 2 + j]
                 lines.append(tiles_all[owner, second[0], second[1]])
             lanes = slice(line * LANES, (line + 1) * LANES)
-            taps_long_out[:, lanes] = jnp.transpose(jnp.concatenate(lines, axis=0))
+            taps_long_out[0, :, lanes] = jnp.transpose(jnp.concatenate(lines, axis=0))
     else:
         outs[0][...] = tiles_own[...]
 
@@ -585,7 +597,7 @@
     smem = pl.BlockSpec(memory_space=pltpu.SMEM)
     tap_count = arrays[3].shape[0]
     if direct:
-        out_shapes = [(1, width), (tap_count, width), (LANES, width // per_group)]
+        out_shapes = [(1, width), (tap_count, 1, width), (1, LANES, width // per_group)]
     else:
         out_shapes = [(sections, tiles) + tile]
     return pl.pallas_call(
@@ -602,7 +614,7 @@
             pltpu.VMEM((sections, ranks, prompt_len, chans), BF16),
             pltpu.VMEM((sections, micro * prompt_len, chans), BF16),
             pltpu.VMEM((sections, 1, chans), F32),
-            pltpu.VMEM((sections, tap_count, chans), F32),
+            pltpu.VMEM((sections, tap_count, 1, chans), F32),
             pltpu.VMEM((sections, group_total, 2 * LANES), F32),
             pltpu.VMEM((sections + 1, rows, chans), BF16),
             pltpu.VMEM((sections, total, micro * chans), BF16),
@@ -686,7 +698,7 @@
         rows,
         prompts,
         norm_gain,
-        short_taps[0],
+        short_taps.transpose(1, 0, 2),
         taps,
         prompt_owner,
         head,
@@ -695,7 +707,7 @@
     )
     scores = scores[:micro, :1].astype(BF16)
     if direct:
-        return (scores, grads[0], grads[1][None], grads[2][None])
+        return (scores, grads[0], grads[1].transpose(1, 0, 2), grads[2])
     grads = lax.psum(grads[0], "resp")
     grads = lax.all_to_all(grads, "section", 0, 0, tiled=True)
     grads = grads.reshape(sections * tiles // 2, 2, 8, LANES)

time: 132 us -> 136 us (1.030)
  Pallas kernels: 123 us -> 127 us
  local copies, waits for them, and re-layouts: 8.03 us -> 6.5 us
    pallas_call x1, Pallas kernels: 123 us -> 127 us  [run_kernel(): pl.pallas_call(functools.partial(kernel, dims, direct), out_shape=(jax.Sh...]
    unnamed x19 -> x14, local copies, waits for them, and re-layouts: 6.63 us -> 5.1 us
where the time goes in v3:
time: 136 us
  Pallas kernels  127 us (93%)
  local copies, waits for them, and re-layouts  6.5 us (5%)
  other arithmetic  1.53 us (1%)
    pallas_call x1, Pallas kernels, run_kernel(): pl.pallas_call(functools.partial(kernel, dims, direct), out_shape=(jax.Sh...  127 us
    unnamed x14, local copies, waits for them, and re-layouts  5.1 us

profile of v3, /device:TPU:0, one launch (start us, length us, event | category | flops | bytes accessed | tf_op | source)
XLA Modules:
  0.0 135.6 jit_solution(14290961762108794353)
XLA Ops:
  0.6 0.0 copy-start.3
  0.6 0.0 copy-start.2
  0.7 0.6 copy-done.3
  1.3 0.6 copy.15.length_ref
  1.9 0.0 copy-done.2
  1.9 0.6 pad.4.ends_ref
  2.5 1.0 copy.13
  3.5 0.1 slice.14
  3.6 0.2 rev.3
  3.8 0.8 pad_maximum_fusion.taps_hbm
  4.7 126.9 %shard_map.120 = (f32[8,128]{1,0:T(8,128)}, f32[1,4096]{1,0:T(1,128)}, f32[7,1,4096]{2,1,0:T(1,128)}, f32[1,128,256]{2,1,0:T(8,128)}) custom-call(bf16[128,4096]{1,0:T(8,128)(2,1)} %bitcast.15, bf16[64,4096]{1,0:T(8,128)(2,1)} %bitcast.16, f32[1,4096]{1,0:T(1,128)} %gain_hbm.1, f32[7,1,4096]{2,1,0:T(1,128)} %bitcast.18, ...), custom_call_target="tpu_custom_call" | custom-call | tf_op jit(solution)/shard_map/pallas_call | solution.py:603
  131.6 0.0 copy-start.1
  131.6 0.7 convert.3
  132.3 0.5 slice.12
  132.8 0.0 copy-done.1
  132.8 0.0 copy-start
  132.8 0.6 copy.21
  133.4 1.6 %copy.22 = f32[1,7,4096]{2,0,1:T(1,128)} copy(f32[1,7,4096]{2,0,1:T(1,128)} %bitcast.17) | data formatting | bytes 229376
  135.0 0.0 copy-done
  135.0 0.7 copy.23
  (1 shorter events, 0.0 us)
Async XLA Ops:
  0.6 0.7 copy-start.3
  0.6 1.3 copy-start.2
  131.6 1.2 copy-start.1
  132.8 2.2 %copy-start = (f32[1,128,256]{2,1,0:T(8,128)S(1)}, f32[1,128,256]{2,1,0:T(8,128)}, u32[]{:S(2)}) copy-start(f32[1,128,256]{2,1,0:T(8,128)} %get-tuple-element.19) | copy-start | bytes 393220

commit v4 on v3

--- a/solution.py
+++ b/solution.py
@@ -213,7 +213,8 @@
     for copy in local_copies:
         copy.start()
     if direct:
-        start_pool(0)
+        for s in range(min(2, sections)):
+            start_pool(s)
     for copy in local_copies:
         copy.wait()
 
@@ -297,9 +298,9 @@
         if direct:
             wait_pool(s)
 
-            @pl.when(s + 1 < sections)
+            @pl.when(s + 2 < sections)
             def _():
-                start_pool(s + 1)
+                start_pool(s + 2)
 
         prompt_acc[...] = jnp.zeros_like(prompt_acc)
         loop(0, blocks, lambda block: choose(s, block))

time: 136 us -> 136 us (level)
  no operation moved by 1% of the time
where the time goes in v4:
time: 136 us; the launch traced here: 135 us
  Pallas kernels  127 us (93%)
  local copies, waits for them, and re-layouts  6.5 us (5%)
  other arithmetic  1.53 us (1%)
    pallas_call x1, Pallas kernels, run_kernel(): pl.pallas_call(functools.partial(kernel, dims, direct), out_shape=(jax.Sh...  127 us
    unnamed x14, local copies, waits for them, and re-layouts  5.1 us

profile of v4, /device:TPU:0, one launch (start us, length us, event | category | flops | bytes accessed | tf_op | source)
XLA Modules:
  0.0 135.2 jit_solution(4584256585395504607)
XLA Ops:
  0.6 0.0 copy-start.3
  0.6 0.0 copy-start.2
  0.7 0.6 copy-done.3
  1.3 0.6 copy.15.length_ref
  1.9 0.0 copy-done.2
  1.9 0.6 pad.4.ends_ref
  2.5 1.0 copy.13
  3.5 0.1 slice.14
  3.6 0.2 rev.3
  3.8 0.8 pad_maximum_fusion.taps_hbm
  4.7 126.5 %shard_map.120 = (f32[8,128]{1,0:T(8,128)}, f32[1,4096]{1,0:T(1,128)}, f32[7,1,4096]{2,1,0:T(1,128)}, f32[1,128,256]{2,1,0:T(8,128)}) custom-call(bf16[128,4096]{1,0:T(8,128)(2,1)} %bitcast.15, bf16[64,4096]{1,0:T(8,128)(2,1)} %bitcast.16, f32[1,4096]{1,0:T(1,128)} %gain_hbm.1, f32[7,1,4096]{2,1,0:T(1,128)} %bitcast.18, ...), custom_call_target="tpu_custom_call" | custom-call | tf_op jit(solution)/shard_map/pallas_call | solution.py:604
  131.2 0.0 copy-start.1
  131.2 0.7 convert.3
  131.9 0.5 slice.12
  132.4 0.0 copy-done.1
  132.4 0.0 copy-start
  132.4 0.6 copy.21
  133.0 1.6 %copy.22 = f32[1,7,4096]{2,0,1:T(1,128)} copy(f32[1,7,4096]{2,0,1:T(1,128)} %bitcast.17) | data formatting | bytes 229376
  134.6 0.0 copy-done
  134.6 0.7 copy.23
  (1 shorter events, 0.0 us)
Async XLA Ops:
  0.6 0.7 copy-start.3
  0.6 1.3 copy-start.2
  131.2 1.2 copy-start.1
  132.4 2.2 %copy-start = (f32[1,128,256]{2,1,0:T(8,128)S(1)}, f32[1,128,256]{2,1,0:T(8,128)}, u32[]{:S(2)}) copy-start(f32[1,128,256]{2,1,0:T(8,128)} %get-tuple-element.19) | copy-start | bytes 393220
